TPU v7x, 256 devices: a whole 4x4x8 slice. The times are simulated.
256 devices in a mesh: mode: 32 (over z_hi, y, core), ex: 4 (over x), ey: 2 (over z_lo).
Axes of the slice: x: 4, y: 4, z: 8 (z_hi: 4, z_lo: 2; z = z_hi * 2 + z_lo), core: 2. Of those that a mesh axis runs over, the one named last changes fastest.
Arguments:
- stream_speed: float32 [12, 12, 16, 4, 2048], P(None, None, 'ex', 'ey', 'mode'), may hold values from -9 to 9, as said below
- normal_speed: float32 [12, 12, 16, 4, 2048], P(None, None, 'ex', 'ey', 'mode'), may hold values from -9 to 9, as said below
Outputs:
- velocity_modes: float32 [12, 12, 16, 4, 4096], P(None, None, 'ex', 'ey', 'mode')
Inputs may be any that keep to these rules, and one draw needn't show every extreme that they name: `stream_speed`: continuous across element faces (shared nodes carry equal values), periodic along the streamwise direction and zero on the walls. `normal_speed`: continuous across element faces (shared nodes carry equal values), periodic along the streamwise direction and zero on the walls.
All inputs are finite; a program needn't handle non-finite values.
Results may differ from a plain program's by a relative error of at most 0.00018.
Values sent between devices are 32-bit elements; how exact they have to be, the bound alone decides.
A program may use at most 128 MiB of HBM per device.

v0:
```python
import functools
import math

import jax
import jax.numpy as jnp
import numpy as np
from jax import lax
from jax.experimental import pallas as pl
from jax.experimental.pallas import tpu as pltpu
from jax.sharding import PartitionSpec as P

P_SIZE = 11
NODES = P_SIZE + 1
FINE = 18
FINE_PAD = 336
ELEMS = 4
ROWS_DEV = 2
ROWS_TOTAL = 4
PLANES = 2048
RANKS = 32
LINE = 24
COLS = 48
GRID = COLS * LINE
FLAT = 1024
EXT_POINTS = NODES + 2
SPECTRAL = ROWS_DEV * EXT_POINTS * 16
WINDOW = EXT_POINTS * LINE
OWN = NODES * LINE

MESH = pl.DeviceIdType.MESH
F32 = jnp.float32
BF16 = jnp.bfloat16

element_width = 2.0
shift_base = 10.0
span_rate = 0.0125


def legendre_pair(degree, points):
    before = points * 0.0 + 1.0
    current = points.copy()
    for step in range(1, degree):
        upcoming = ((2 * step + 1) * points * current - step * before) / (step + 1)
        before = current
        current = upcoming
    return (current, before)


def legendre_slope(degree, points):
    current, before = legendre_pair(degree, points)
    return (current, degree * (points * current - before) / (points * points - 1.0))


def lobatto_points(order):
    guesses = -np.cos(np.pi * np.arange(1, order) / order)
    for step in range(60):
        current, slope = legendre_slope(order, guesses)
        second = (2.0 * guesses * slope - order * (order + 1) * current) / (1.0 - guesses * guesses)
        guesses = guesses - slope / second
    return guesses


def gauss_rule(count):
    guesses = -np.cos(np.pi * (np.arange(count) + 0.75) / (count + 0.5))
    for step in range(60):
        current, slope = legendre_slope(count, guesses)
        guesses = guesses - current / slope
    current, slope = legendre_slope(count, guesses)
    return (guesses, 2.0 / ((1.0 - guesses * guesses) * slope * slope))


def jacobi_eigen(matrix):
    size_n = matrix.shape[0]
    work = matrix.copy()
    vectors = np.eye(size_n)
    for sweep_number in range(20):
        for first in range(size_n):
            for second in range(first + 1, size_n):
                coupling = work[first, second]
                if abs(coupling) > 1e-300:
                    theta = (work[second, second] - work[first, first]) / (2.0 * coupling)
                    direction = 1.0 if theta >= 0.0 else -1.0
                    tangent = direction / (abs(theta) + np.sqrt(theta * theta + 1.0))
                    cosine = 1.0 / np.sqrt(tangent * tangent + 1.0)
                    sine = tangent * cosine
                    rotation = np.eye(size_n)
                    rotation[first, first] = cosine
                    rotation[second, second] = cosine
                    rotation[first, second] = sine
                    rotation[second, first] = -sine
                    work = rotation.T @ work @ rotation
                    vectors = vectors @ rotation
    diagonal_index = np.arange(size_n)
    return (work[diagonal_index, diagonal_index], vectors)


def extended_basis(stiffness, weights, left_width, centre_width, right_width):
    node_count = weights.shape[0]
    full_count = 3 * node_count - 2
    stiff_full = np.zeros((full_count, full_count))
    mass_full = np.zeros(full_count)
    for position, span_width in enumerate((left_width, centre_width, right_width)):
        if span_width > 0.0:
            first_node = position * (node_count - 1)
            stiff_full[
                first_node : first_node + node_count, first_node : first_node + node_count
            ] += stiffness * (2.0 / span_width)
            mass_full[first_node : first_node + node_count] += weights * (span_width / 2.0)
    low_index = node_count - 2
    high_index = low_index + node_count + 2
    stiff_ext = stiff_full[low_index:high_index, low_index:high_index].copy()
    mass_ext = mass_full[low_index:high_index].copy()
    frozen_list = []
    if left_width <= 0.0:
        frozen_list += [0, 1]
    if right_width <= 0.0:
        frozen_list += [node_count, node_count + 1]
    for frozen_index in frozen_list:
        stiff_ext[frozen_index, :] = 0.0
        stiff_ext[:, frozen_index] = 0.0
        stiff_ext[frozen_index, frozen_index] = 1.0
        mass_ext[frozen_index] = 1.0
    inverse_root = 1.0 / np.sqrt(mass_ext)
    lambdas, vectors = jacobi_eigen(inverse_root[:, None] * stiff_ext * inverse_root[None, :])
    return (inverse_root[:, None] * vectors, lambdas)


def spectral_tables(order, rows_total):
    inner_points = lobatto_points(order)
    points = np.concatenate([[-1.0], inner_points, [1.0]])
    values, unused_before = legendre_pair(order, points)
    weights = 2.0 / (order * (order + 1) * values**2)
    identity = np.eye(order + 1)
    point_gaps = points[:, None] - points[None, :] + identity
    derivative = values[:, None] / (values[None, :] * point_gaps) * (1.0 - identity)
    derivative[0, 0] = -order * (order + 1) / 4.0
    derivative[order, order] = order * (order + 1) / 4.0
    stiffness = derivative.T @ (weights[:, None] * derivative)
    gauss_points, gauss_weights = gauss_rule(3 * (order + 1) // 2)
    offsets = gauss_points[:, None, None] - points[None, None, :]
    numerators = np.prod(np.where(identity[None, :, :] > 0.5, 1.0, offsets), axis=2)
    denominators = np.prod(np.where(identity > 0.5, 1.0, points[:, None] - points[None, :]), axis=1)
    interp = numerators / denominators[None, :]
    heights = 0.6 + 1.4 * np.sin(np.pi * (np.arange(rows_total) + 0.5) / rows_total)
    basis_x, lambdas_x = extended_basis(
        stiffness, weights, element_width, element_width, element_width
    )
    basis_rows = []
    lambda_rows = []
    for row_number in range(rows_total):
        below = heights[row_number - 1] if row_number > 0 else 0.0
        above = heights[row_number + 1] if row_number < rows_total - 1 else 0.0
        basis_one, lambda_one = extended_basis(
            stiffness, weights, below, heights[row_number], above
        )
        basis_rows.append(basis_one)
        lambda_rows.append(lambda_one)
    return (
        derivative,
        interp,
        gauss_weights,
        weights,
        stiffness,
        basis_x,
        lambdas_x,
        np.stack(basis_rows),
        np.stack(lambda_rows),
        heights,
    )


def bf16_pair(table):
    high = np.asarray(table, np.float32).astype(BF16)
    low = (np.asarray(table, np.float64) - high.astype(np.float64)).astype(np.float32)
    return high, low.astype(BF16)


def split(value):
    high = value.astype(BF16)
    return high, (value - high.astype(F32)).astype(BF16)


def dot(left, right):
    return jnp.dot(left, right, preferred_element_type=F32)


def dot_rows(left, right):
    return lax.dot_general(left, right, (((1,), (1,)), ((), ())), preferred_element_type=F32)


@functools.cache
def all_tables():
    (derivative, interp, gauss_weights, weights, stiffness, basis_x, lambdas_x, basis_y,
     lambdas_y, heights) = spectral_tables(P_SIZE, ROWS_TOTAL)
    nodes = NODES * NODES
    fine = FINE * FINE
    lift = np.zeros((3, FINE_PAD, nodes))
    lift[0, :fine] = np.kron(interp, interp)
    lift[1, :fine] = np.kron(interp @ derivative * (2.0 / element_width), interp)
    lift[2, :fine] = np.kron(interp, interp @ derivative)
    lift = lift.reshape(3 * FINE_PAD, nodes)
    lift_high, lift_low = bf16_pair(lift)
    lift_cat = np.concatenate([lift_high, lift_high, lift_low], 1)
    back = np.zeros((NODES, LINE, ROWS_DEV, FINE_PAD))
    quad = np.kron(gauss_weights, gauss_weights)
    back_one = -(np.kron(interp.T, interp.T) * quad[None, :]).reshape(NODES, NODES, fine)
    for f in range(ROWS_DEV):
        back[:, P_SIZE * f : P_SIZE * f + NODES, f, :fine] += back_one
    back_high, back_low = bf16_pair(back.reshape(NODES * LINE, ROWS_DEV * FINE_PAD))
    plane = np.arange(64)[None, :]
    fourier = np.zeros((16, 2, 2, 32, 2, 64))
    for rp in range(16):
        for half in range(2):
            r = rp if half == 0 else (32 - rp if rp else 16)
            mode = 32 * np.arange(32)[:, None] + r
            angle = 2.0 * np.pi * ((mode * plane) % PLANES) / PLANES
            cosine, sine = np.cos(angle) / PLANES, np.sin(angle) / PLANES
            if rp == 0:
                fourier[rp, half, 0, :, half] = cosine
                fourier[rp, half, 1, :, half] = -sine
            else:
                sign = 1.0 if half == 0 else -1.0
                fourier[rp, half, 0, :, 0] = cosine
                fourier[rp, half, 0, :, 1] = sign * sine
                fourier[rp, half, 1, :, 0] = -sine
                fourier[rp, half, 1, :, 1] = sign * cosine
    four_high, four_low = bf16_pair(fourier.reshape(16, 128, 128))
    four_cat = np.concatenate([four_high, four_low], 2)
    line_basis = np.zeros((2, ROWS_DEV, LINE, 16))
    line_lambda = np.ones((2, ROWS_DEV, 16))
    line_mass = np.zeros((2, LINE))
    line_stiff = np.zeros((2, LINE, LINE))
    top = P_SIZE * ROWS_TOTAL
    for ey in range(2):
        low = 21 * ey
        for f in range(ROWS_DEV):
            row = ROWS_DEV * ey + f
            line_lambda[ey, f, :EXT_POINTS] = lambdas_y[row]
            for b in range(EXT_POINTS):
                g = P_SIZE * row + b - 1
                if 0 < g < top:
                    line_basis[ey, f, g - low, :EXT_POINTS] = basis_y[row, b]
            for b in range(NODES):
                g = P_SIZE * row + b
                if 0 < g < top:
                    line_mass[ey, g - low] += heights[row] / 2.0 * weights[b]
                    for c in range(NODES):
                        h = P_SIZE * row + c
                        if 0 < h < top:
                            line_stiff[ey, g - low, h - low] += 2.0 / heights[row] * stiffness[b, c]
    ones_line = np.ones(LINE)
    in_x = np.kron(basis_x.T, ones_line[None, :])
    in_y = np.tile(np.transpose(line_basis, (0, 1, 3, 2)), (1, 1, 1, EXT_POINTS))
    out_x = np.tile(np.kron(basis_x, np.ones((1, 16))), (1, ROWS_DEV))
    out_y = np.concatenate(
        [np.tile(line_basis[:, f], (1, 1, EXT_POINTS)) for f in range(ROWS_DEV)], 2)
    eye = np.eye(NODES)
    own_kx = np.kron(stiffness * (2.0 / element_width), ones_line[None, :])
    own_my = np.tile(line_mass[:, :, None] * np.eye(LINE)[None], (1, 1, NODES))
    own_wx = np.kron(np.diag(weights) * (element_width / 2.0), ones_line[None, :])
    own_ky = np.tile(line_stiff, (1, 1, NODES))
    wide = np.ones((1, 1, 128))
    single = dict(
        lift=lift_cat, back_high=back_high, back_low=back_low, fourier=four_cat)
    single.update({name: np.asarray(table, np.float32) for name, table in dict(
        in_x=in_x, in_y=in_y, out_x=out_x, out_y=out_y,
        own_kx=own_kx, own_my=own_my, own_wx=own_wx, own_ky=own_ky,
        mass=line_mass[:, :, None] * wide, lam=line_lambda[..., None] * wide[None]).items()})
    return single, np.asarray(lambdas_x), np.asarray(weights), np.asarray(heights)


def advect_kernel(heights, u_ref, v_ref, lift_ref, high_ref, low_ref, out_ref):
    ey = lax.axis_index("ey")
    lane = lax.broadcasted_iota(jnp.int32, (FINE_PAD, 128), 1)
    first = lane < 64
    products = []
    for f in range(ROWS_DEV):
        columns = []
        for e in range(ELEMS):
            rows = pl.ds(ROWS_DEV * e + f, NODES * NODES, stride=ROWS_DEV * ELEMS)
            columns.append(jnp.concatenate([u_ref[rows, :], v_ref[rows, :]], 1))
        high, low = split(jnp.concatenate(columns, 1))
        fine = dot(lift_ref[...], jnp.concatenate([high, low, high], 0))
        half_height = jnp.where(
            ey == 0, np.float32(heights[f] / 2.0), np.float32(heights[ROWS_DEV + f] / 2.0))
        parts = []
        for e in range(ELEMS):
            block = slice(128 * e, 128 * e + 128)
            speed = fine[:FINE_PAD, block]
            turned = pltpu.roll(speed, 64, 1)
            along = jnp.where(first, speed, turned) * half_height
            across = jnp.where(first, turned, speed)
            parts.append(
                along * fine[FINE_PAD : 2 * FINE_PAD, block] + across * fine[2 * FINE_PAD :, block])
        products.append(jnp.concatenate(parts, 1))
    high, low = split(jnp.concatenate(products, 0))
    weak = dot(high_ref[...], high) + dot(high_ref[...], low) + dot(low_ref[...], high)
    weak = jnp.where(ey == 0, pltpu.roll(weak, OWN - 1, 0), weak)
    for e in range(ELEMS):
        for a in range(NODES):
            if a == P_SIZE and e < ELEMS - 1:
                continue
            value = weak[LINE * a : LINE * a + 22, 128 * e : 128 * e + 128]
            if a == 0 and e > 0:
                value += weak[LINE * P_SIZE : LINE * P_SIZE + 22, 128 * e - 128 : 128 * e]
            x = P_SIZE * e + a
            out_ref[22 * x : 22 * x + 22, :] = value
    out_ref[990:, :] = jnp.zeros((FLAT - 990, 128), F32)


def real_transform(values):
    count = len(values)
    if count == 1:
        return [(values[0], None)]
    if count == 2:
        return [(values[0] + values[1], None), (values[0] - values[1], None)]
    even, odd = real_transform(values[0::2]), real_transform(values[1::2])
    quarter, half = count // 4, count // 2
    result = []
    for r in range(half + 1):
        s = r % half

        def pick(part):
            if s <= quarter:
                return part[s], 1.0
            return part[half - s], -1.0

        (er, ei), es = pick(even)
        (dr, di), ds = pick(odd)
        c, n = math.cos(2 * math.pi * r / count), -math.sin(2 * math.pi * r / count)
        if r == 0:
            result.append((er + dr, None))
        elif r == half:
            result.append((er - dr, None))
        elif 4 * r == count:
            result.append((er, -dr))
        else:
            c, n = np.float32(c), np.float32(n)
            if di is None:
                tr, ti = dr * c, dr * n
            else:
                tr = dr * c - di * (n * np.float32(ds))
                ti = dr * n + di * (c * np.float32(ds))
            result.append((er + tr, ti if ei is None else (ti + ei if es > 0 else ti - ei)))
    return result


def transform_kernel(in_ref, table_ref, out_ref, mid_ref, turn_ref):
    for block in range(4):
        rows = slice(8 * block, 8 * block + 8)
        values = [in_ref[32 * d + 8 * block : 32 * d + 8 * block + 8, :] for d in range(RANKS)]
        found = real_transform(values)
        for r in range(1, 16):
            mid_ref[2 * r, rows, :], mid_ref[2 * r + 1, rows, :] = found[r]
        mid_ref[0, rows, :] = found[0][0]
        mid_ref[1, rows, :] = found[16][0]
    first = lax.broadcasted_iota(jnp.int32, (32, 128), 1) < 64
    for rp in range(16):
        real, imag = mid_ref[2 * rp], mid_ref[2 * rp + 1]
        both = jnp.concatenate(
            [jnp.where(first, real, pltpu.roll(imag, 64, 1)),
             jnp.where(first, pltpu.roll(real, 64, 1), imag)], 0)
        high, low = split(both)
        table = table_ref[rp]
        found = dot_rows(table, jnp.concatenate([high, high], 1)) + dot_rows(table[:, :128], low)
        for half in range(2):
            r = rp if half == 0 else (32 - rp if rp else 16)
            for c in range(2):
                start = 32 * (2 * half + c)
                for k in range(2):
                    turn_ref[pl.ds(4 * r + 2 * c + k, 32, stride=128), :] = found[start : start + 32, :]
    even = lax.broadcasted_iota(jnp.int32, (32, 128), 1) % 2 == 0
    for q in range(RANKS):
        turned = turn_ref[128 * q : 128 * q + 128, :].T
        out_ref[32 * q : 32 * q + 32, :] = jnp.where(even, turned[:32], turned[32:])


def share_kernel(in_ref, out_ref, send_sem, recv_sem):
    me = lax.axis_index("mode")
    barrier = pltpu.get_barrier_semaphore()

    def signal(i, carry):
        pl.semaphore_signal(
            barrier, inc=1, device_id={"mode": lax.rem(me + i, RANKS)}, device_id_type=MESH)
        return carry

    lax.fori_loop(1, RANKS, signal, 0)
    pl.semaphore_wait(barrier, RANKS - 1)

    def copy(i):
        peer = lax.rem(me + i, RANKS)
        return pltpu.make_async_remote_copy(
            src_ref=in_ref.at[pl.ds(pl.multiple_of(32 * peer, 32), 32)],
            dst_ref=out_ref.at[pl.ds(pl.multiple_of(32 * me, 32), 32)],
            send_sem=send_sem.at[i],
            recv_sem=recv_sem.at[i],
            device_id={"mode": peer},
            device_id_type=MESH,
        )

    def start(i, carry):
        copy(i).start()
        return carry

    def finish(i, carry):
        copy(i).wait()
        return carry

    lax.fori_loop(1, RANKS, start, 0)
    mine = pl.ds(pl.multiple_of(32 * me, 32), 32)
    out_ref[mine, :] = in_ref[mine, :]
    lax.fori_loop(1, RANKS, finish, 0)


RESIDUAL = ((1, 44, 45, 0), (21, 22), (1, 0))
CORRECTION = ((0, 45, 44, 1), (22, 21), (0, 1))


def smooth_kernel(
    lambdas_x, weights, flat_ref, in_x, in_y, out_x, out_y, own_kx, own_my, own_wx, own_ky, mass_ref,
    lam_ref, out_ref, inward, outward, local, inverse, raw, field, fix, total, side, line, corner,
    side_in, line_in, corner_in, send_sem, recv_sem):
    ey = lax.axis_index("ey")
    ex = lax.axis_index("ex")
    left, right = lax.rem(ex + 3, 4), lax.rem(ex + 1, 4)
    other = 1 - ey
    low_side = ey == 0
    peers = ({"ex": left}, {"ex": right}, {"ey": other},
             {"ex": left, "ey": other}, {"ex": right, "ey": other})
    barrier = pltpu.get_barrier_semaphore()
    for peer in peers:
        pl.semaphore_signal(barrier, inc=1, device_id=peer, device_id_type=MESH)

    raw[...] = jnp.zeros((GRID, 128), F32)
    for x in range(45):
        raw[LINE * (x + 1) + 1 : LINE * (x + 1) + 23, :] = flat_ref[22 * x : 22 * x + 22, :]

    lane = lax.broadcasted_iota(jnp.int32, (1, 128), 1)
    mode = (lax.axis_index("mode") * 32 + lane // 4).astype(F32)
    shift = shift_base + (np.float32(span_rate) * mode) ** 2
    for f in range(ROWS_DEV):
        for i in range(EXT_POINTS):
            row = 16 * (EXT_POINTS * f + i)
            high, low = split(in_x[i : i + 1, :] * in_y[ey, f])
            inward[0, row : row + 16, :] = high
            inward[1, row : row + 16, :] = low
            inverse[row : row + 16, :] = 1.0 / (lam_ref[ey, f] + (shift + np.float32(lambdas_x[i])))
    high, low = split(jnp.concatenate([out_x[a : a + 1, :] * out_y[ey] for a in range(EXT_POINTS)], 0))
    outward[0], outward[1] = high, low
    high, low = split(jnp.concatenate(
        [own_kx[a : a + 1, :] * own_my[ey] + own_wx[a : a + 1, :] * own_ky[ey] for a in range(NODES)], 0))
    local[0], local[1] = high, low

    pl.semaphore_wait(barrier, 5)

    def exchange(number, grid, kind):
        (to_left, to_right, from_right, from_left), lower, upper = kind
        side[number, 0] = grid[LINE * to_left : LINE * to_left + 48, :]
        side[number, 1] = grid[LINE * to_right : LINE * to_right + 48, :]
        zero = jnp.zeros((4, 128), F32)
        pieces = []
        for step in range(2):
            rows = jnp.where(
                low_side,
                grid[pl.ds(lower[0] + step, COLS, stride=LINE), :],
                grid[pl.ds(upper[0] + step, COLS, stride=LINE), :])
            line[number, step] = rows
            pieces.append(rows)
        for at, column in enumerate((to_left, to_right)):
            corner[number, at] = jnp.concatenate([p[column : column + 2] for p in pieces] + [zero], 0)
        sends = (
            (side.at[number, 0], side_in.at[number, 0]),
            (side.at[number, 1], side_in.at[number, 1]),
            (line.at[number], line_in.at[number]),
            (corner.at[number, 0], corner_in.at[number, 0]),
            (corner.at[number, 1], corner_in.at[number, 1]))
        copies = []
        for at, ((source, target), peer) in enumerate(zip(sends, peers, strict=True)):
            copies.append(pltpu.make_async_remote_copy(
                src_ref=source, dst_ref=target, send_sem=send_sem.at[number, at],
                recv_sem=recv_sem.at[number, at], device_id=peer, device_id_type=MESH))
            copies[-1].start()
        for sent in copies:
            sent.wait()
        grid[LINE * from_right : LINE * from_right + 48, :] += side_in[number, 0]
        grid[LINE * from_left : LINE * from_left + 48, :] += side_in[number, 1]
        zeros = jnp.zeros((COLS, 128), F32)
        for step in range(2):
            rows = [line_in[number, step]]
            for at, column in enumerate((from_right, from_left)):
                piece = corner_in[number, at, 2 * step : 2 * step + 2, :]
                before = [jnp.zeros((column, 128), F32)] if column else []
                rows.append(jnp.concatenate(
                    before + [piece, jnp.zeros((COLS - 2 - column, 128), F32)], 0))
            added = rows[0] + rows[1] + rows[2]
            where_low = pl.ds(lower[1] + step, COLS, stride=LINE)
            where_up = pl.ds(upper[1] + step, COLS, stride=LINE)
            grid[where_low, :] += jnp.where(low_side, added, zeros)
            grid[where_up, :] += jnp.where(low_side, zeros, added)

    def solve(source, target):
        value = jnp.concatenate(
            [source[264 * e : 264 * e + WINDOW, :] for e in range(ELEMS)], 1)
        high, low = split(value)
        modal = dot(inward[0], high) + dot(inward[0], low) + dot(inward[1], high)
        modal = modal * jnp.concatenate([inverse[...]] * ELEMS, 1)
        high, low = split(modal)
        back = dot(outward[0], high) + dot(outward[0], low) + dot(outward[1], high)
        target[...] = jnp.zeros((GRID, 128), F32)
        for e in range(ELEMS):
            target[264 * e : 264 * e + WINDOW, :] += back[:, 128 * e : 128 * e + 128]

    field[...] = raw[...]
    exchange(0, field, RESIDUAL)
    solve(field, total)
    exchange(1, total, CORRECTION)
    value = jnp.concatenate(
        [total[264 * e + LINE : 264 * e + LINE + OWN, :] for e in range(ELEMS)], 1)
    high, low = split(value)
    applied = dot(local[0], high) + dot(local[0], low) + dot(local[1], high)
    coefficient = jnp.concatenate(
        [(np.float32(weights[a] * element_width / 2.0) * shift) * mass_ref[ey] for a in range(NODES)], 0)
    applied = applied + value * jnp.concatenate([coefficient] * ELEMS, 1)
    field[...] = raw[...]
    for e in range(ELEMS):
        field[264 * e + LINE : 264 * e + LINE + OWN, :] -= applied[:, 128 * e : 128 * e + 128]
    exchange(2, field, RESIDUAL)
    solve(field, fix)
    exchange(3, fix, CORRECTION)
    total[...] += fix[...]
    for e in range(ELEMS):
        for f in range(ROWS_DEV):
            for a in range(NODES):
                start = LINE * (P_SIZE * e + 1 + a) + P_SIZE * f
                out_ref[pl.ds(96 * a + 2 * e + f, NODES, stride=8), :] = jnp.where(
                    low_side, total[start : start + NODES, :], total[start + 1 : start + 1 + NODES, :])


def on_device(stream_speed, normal_speed):
    single, lambdas_x, weights, heights = all_tables()
    vmem = pl.BlockSpec(memory_space=pltpu.VMEM)
    flat = jax.ShapeDtypeStruct((FLAT, 128), F32)

    def share(value, number):
        return pl.pallas_call(
            share_kernel,
            out_shape=flat,
            in_specs=[vmem],
            out_specs=vmem,
            scratch_shapes=[pltpu.SemaphoreType.DMA((RANKS,)), pltpu.SemaphoreType.DMA((RANKS,))],
            compiler_params=pltpu.CompilerParams(collective_id=number, has_side_effects=True),
            name=f"share_{number}",
        )(value)

    tables = {name: jnp.asarray(table) for name, table in single.items()}
    weak = pl.pallas_call(
        functools.partial(advect_kernel, heights),
        out_shape=flat,
        in_specs=[vmem] * 5,
        out_specs=vmem,
        name="advect",
    )(stream_speed.reshape(1152, 64), normal_speed.reshape(1152, 64), tables["lift"],
      tables["back_high"], tables["back_low"])
    spectra = pl.pallas_call(
        transform_kernel,
        out_shape=flat,
        in_specs=[vmem] * 2,
        out_specs=vmem,
        scratch_shapes=[pltpu.VMEM((32, 32, 128), F32), pltpu.VMEM((4096, 64), F32)],
        name="transform",
    )(share(weak, 1), tables["fourier"])
    names = ("in_x", "in_y", "out_x", "out_y", "own_kx", "own_my", "own_wx", "own_ky", "mass", "lam")
    grid = pltpu.VMEM((GRID, 128), F32)
    solved = pl.pallas_call(
        functools.partial(smooth_kernel, lambdas_x, weights),
        out_shape=jax.ShapeDtypeStruct((1152, 128), F32),
        in_specs=[vmem] * (1 + len(names)),
        out_specs=vmem,
        scratch_shapes=[
            pltpu.VMEM((2, SPECTRAL, WINDOW), BF16),
            pltpu.VMEM((2, WINDOW, SPECTRAL), BF16),
            pltpu.VMEM((2, OWN, OWN), BF16),
            pltpu.VMEM((SPECTRAL, 128), F32),
            grid, grid, grid, grid,
            pltpu.VMEM((4, 2, 48, 128), F32),
            pltpu.VMEM((4, 2, COLS, 128), F32),
            pltpu.VMEM((4, 2, 8, 128), F32),
            pltpu.VMEM((4, 2, 48, 128), F32),
            pltpu.VMEM((4, 2, COLS, 128), F32),
            pltpu.VMEM((4, 2, 8, 128), F32),
            pltpu.SemaphoreType.DMA((4, 5)),
            pltpu.SemaphoreType.DMA((4, 5)),
        ],
        compiler_params=pltpu.CompilerParams(collective_id=3, has_side_effects=True),
        name="smooth",
    )(share(spectra, 2), *[tables[name] for name in names])
    return solved.reshape(12, 12, 4, 2, 128)


def solution(mesh):
    return jax.shard_map(
        on_device,
        mesh=mesh,
        in_specs=(P(None, None, "ex", "ey", "mode"), P(None, None, "ex", "ey", "mode")),
        out_specs=P(None, None, "ex", "ey", "mode"),
        check_vma=False,
    )
```

profile of v0, /device:TPU:24, one launch (start us, length us, event | category | flops | bytes accessed | tf_op | source)
XLA Modules:
  0.0 86.7 jit_solution(1920016588617128077)
XLA Ops:
  0.0 4.8 %advect.1.in_ref = f32[1024,128]{1,0:T(8,128)} custom-call(f32[1152,64]{1,0:T(8,128)} %bitcast.4, f32[1152,64]{1,0:T(8,128)} %bitcast.5, bf16[1008,432]{1,0:T(8,128)(2,1)} %constant.28.clone.lift_ref, bf16[288,672]{1,0:T(8,128)(2,1)} %constant.29.clone.high_ref, bf16[288,672]{1,0:T(8,128)(2,1)} %constant.30.clone.low_ref), custom_call_target="tpu_custom_call" | custom-call | tf_op jit(solution)/shard_map/advect/pallas_call | solution.py:556
  4.8 23.9 %share_1.1.in_ref = f32[1024,128]{1,0:T(8,128)} custom-call(f32[1024,128]{1,0:T(8,128)} %advect.1.in_ref), custom_call_target="tpu_custom_call" | custom-call | tf_op jit(solution)/shard_map/share_1/pallas_call | solution.py:545
  28.7 4.6 %transform.1.in_ref = f32[1024,128]{1,0:T(8,128)} custom-call(f32[1024,128]{1,0:T(8,128)} %share_1.1.in_ref, bf16[16,128,256]{2,1,0:T(8,128)(2,1)} %constant.31.clone.table_ref), custom_call_target="tpu_custom_call" | custom-call | tf_op jit(solution)/shard_map/transform/pallas_call | solution.py:564
  33.3 25.0 %share_2.1.flat_ref = f32[1024,128]{1,0:T(8,128)} custom-call(f32[1024,128]{1,0:T(8,128)} %transform.1.in_ref), custom_call_target="tpu_custom_call" | custom-call | tf_op jit(solution)/shard_map/share_2/pallas_call | solution.py:545
  58.3 26.3 %smooth.1 = f32[1152,128]{1,0:T(8,128)} custom-call(f32[1024,128]{1,0:T(8,128)} %share_2.1.flat_ref, f32[14,336]{1,0:T(8,128)} %constant.32.clone.in_x, f32[2,2,16,336]{3,2,1,0:T(8,128)} %constant.33.clone.in_y, f32[14,448]{1,0:T(8,128)} %constant.34.clone.out_x, f32[2,24,448]{2,1,0:T(8,128)} %constant.35.clone.out_y, f32[12,288]{1,0:T(8,128)} %constant.36.clone.own_kx, ...), custom_call_target="tpu_custom_call" | custom-call | tf_op jit(solution)/shard_map/smooth/pallas_call | solution.py:574
  84.6 2.1 %copy.18 = f32[12,12,4,2,128]{4,3,2,1,0:T(2,128)} copy(f32[12,12,4,2,128]{4,3,2,1,0:T(2,128)} %bitcast.3) | data formatting | bytes 1179648
where the time goes:
time: 87 us; the launch traced here: 86.7 us
  Pallas kernels  84.6 us (97%)
  local copies, waits for them, and re-layouts  2.08 us (2%)
    pallas_call x2, Pallas kernels, share(): pl.pallas_call(share_kernel, out_shape=flat, in_specs=[vmem], out_specs=v...  48.9 us
    pallas_call x1, Pallas kernels, on_device(): pl.pallas_call(functools.partial(smooth_kernel, lambdas_x, weights), out_...  26.3 us
    pallas_call x1, Pallas kernels, on_device(): pl.pallas_call(functools.partial(advect_kernel, heights), out_shape=flat,...  4.82 us
    pallas_call x1, Pallas kernels, on_device(): pl.pallas_call(transform_kernel, out_shape=flat, in_specs=[vmem] * 2, out...  4.61 us
    unnamed x1, local copies, waits for them, and re-layouts  2.08 us

commit v1 on v0

--- a/solution.py
+++ b/solution.py
@@ -208,24 +208,25 @@
         back[:, P_SIZE * f : P_SIZE * f + NODES, f, :fine] += back_one
     back_high, back_low = bf16_pair(back.reshape(NODES * LINE, ROWS_DEV * FINE_PAD))
     plane = np.arange(64)[None, :]
-    fourier = np.zeros((16, 2, 2, 32, 2, 64))
+    angle = 2.0 * np.pi * ((np.arange(32)[:, None] * plane) % 64) / 64.0
+    wave = np.tile(np.stack([np.cos(angle), np.sin(angle)]), (1, 1, 2))
+    twist = np.zeros((16, 4, 2, 2, 64))
     for rp in range(16):
         for half in range(2):
             r = rp if half == 0 else (32 - rp if rp else 16)
-            mode = 32 * np.arange(32)[:, None] + r
-            angle = 2.0 * np.pi * ((mode * plane) % PLANES) / PLANES
-            cosine, sine = np.cos(angle) / PLANES, np.sin(angle) / PLANES
+            turn = 2.0 * np.pi * r * np.arange(64) / PLANES
+            cosine = np.stack([np.cos(turn), -np.sin(turn)]) / PLANES
+            sine = np.stack([np.sin(turn), np.cos(turn)]) / PLANES
             if rp == 0:
-                fourier[rp, half, 0, :, half] = cosine
-                fourier[rp, half, 1, :, half] = -sine
+                twist[rp, 2 * half, :, half] = cosine
+                twist[rp, 2 * half + 1, :, half] = -sine
             else:
                 sign = 1.0 if half == 0 else -1.0
-                fourier[rp, half, 0, :, 0] = cosine
-                fourier[rp, half, 0, :, 1] = sign * sine
-                fourier[rp, half, 1, :, 0] = -sine
-                fourier[rp, half, 1, :, 1] = sign * cosine
-    four_high, four_low = bf16_pair(fourier.reshape(16, 128, 128))
-    four_cat = np.concatenate([four_high, four_low], 2)
+                twist[rp, 2 * half, :, 0] = cosine
+                twist[rp, 2 * half, :, 1] = sign * sine
+                twist[rp, 2 * half + 1, :, 0] = -sine
+                twist[rp, 2 * half + 1, :, 1] = sign * cosine
+    twist = twist.reshape(16, 8, 128)
     line_basis = np.zeros((2, ROWS_DEV, LINE, 16))
     line_lambda = np.ones((2, ROWS_DEV, 16))
     line_mass = np.zeros((2, LINE))
@@ -260,52 +261,13 @@
     own_wx = np.kron(np.diag(weights) * (element_width / 2.0), ones_line[None, :])
     own_ky = np.tile(line_stiff, (1, 1, NODES))
     wide = np.ones((1, 1, 128))
-    single = dict(
-        lift=lift_cat, back_high=back_high, back_low=back_low, fourier=four_cat)
+    single = dict(lift=lift_cat, back_high=back_high, back_low=back_low)
     single.update({name: np.asarray(table, np.float32) for name, table in dict(
+        wave=wave, twist=twist,
         in_x=in_x, in_y=in_y, out_x=out_x, out_y=out_y,
         own_kx=own_kx, own_my=own_my, own_wx=own_wx, own_ky=own_ky,
         mass=line_mass[:, :, None] * wide, lam=line_lambda[..., None] * wide[None]).items()})
     return single, np.asarray(lambdas_x), np.asarray(weights), np.asarray(heights)
-
-
-def advect_kernel(heights, u_ref, v_ref, lift_ref, high_ref, low_ref, out_ref):
-    ey = lax.axis_index("ey")
-    lane = lax.broadcasted_iota(jnp.int32, (FINE_PAD, 128), 1)
-    first = lane < 64
-    products = []
-    for f in range(ROWS_DEV):
-        columns = []
-        for e in range(ELEMS):
-            rows = pl.ds(ROWS_DEV * e + f, NODES * NODES, stride=ROWS_DEV * ELEMS)
-            columns.append(jnp.concatenate([u_ref[rows, :], v_ref[rows, :]], 1))
-        high, low = split(jnp.concatenate(columns, 1))
-        fine = dot(lift_ref[...], jnp.concatenate([high, low, high], 0))
-        half_height = jnp.where(
-            ey == 0, np.float32(heights[f] / 2.0), np.float32(heights[ROWS_DEV + f] / 2.0))
-        parts = []
-        for e in range(ELEMS):
-            block = slice(128 * e, 128 * e + 128)
-            speed = fine[:FINE_PAD, block]
-            turned = pltpu.roll(speed, 64, 1)
-            along = jnp.where(first, speed, turned) * half_height
-            across = jnp.where(first, turned, speed)
-            parts.append(
-                along * fine[FINE_PAD : 2 * FINE_PAD, block] + across * fine[2 * FINE_PAD :, block])
-        products.append(jnp.concatenate(parts, 1))
-    high, low = split(jnp.concatenate(products, 0))
-    weak = dot(high_ref[...], high) + dot(high_ref[...], low) + dot(low_ref[...], high)
-    weak = jnp.where(ey == 0, pltpu.roll(weak, OWN - 1, 0), weak)
-    for e in range(ELEMS):
-        for a in range(NODES):
-            if a == P_SIZE and e < ELEMS - 1:
-                continue
-            value = weak[LINE * a : LINE * a + 22, 128 * e : 128 * e + 128]
-            if a == 0 and e > 0:
-                value += weak[LINE * P_SIZE : LINE * P_SIZE + 22, 128 * e - 128 : 128 * e]
-            x = P_SIZE * e + a
-            out_ref[22 * x : 22 * x + 22, :] = value
-    out_ref[990:, :] = jnp.zeros((FLAT - 990, 128), F32)
 
 
 def real_transform(values):
@@ -345,118 +307,206 @@
     return result
 
 
-def transform_kernel(in_ref, table_ref, out_ref, mid_ref, turn_ref):
-    for block in range(4):
-        rows = slice(8 * block, 8 * block + 8)
-        values = [in_ref[32 * d + 8 * block : 32 * d + 8 * block + 8, :] for d in range(RANKS)]
-        found = real_transform(values)
-        for r in range(1, 16):
-            mid_ref[2 * r, rows, :], mid_ref[2 * r + 1, rows, :] = found[r]
-        mid_ref[0, rows, :] = found[0][0]
-        mid_ref[1, rows, :] = found[16][0]
-    first = lax.broadcasted_iota(jnp.int32, (32, 128), 1) < 64
-    for rp in range(16):
-        real, imag = mid_ref[2 * rp], mid_ref[2 * rp + 1]
-        both = jnp.concatenate(
-            [jnp.where(first, real, pltpu.roll(imag, 64, 1)),
-             jnp.where(first, pltpu.roll(real, 64, 1), imag)], 0)
-        high, low = split(both)
-        table = table_ref[rp]
-        found = dot_rows(table, jnp.concatenate([high, high], 1)) + dot_rows(table[:, :128], low)
-        for half in range(2):
-            r = rp if half == 0 else (32 - rp if rp else 16)
-            for c in range(2):
-                start = 32 * (2 * half + c)
-                for k in range(2):
-                    turn_ref[pl.ds(4 * r + 2 * c + k, 32, stride=128), :] = found[start : start + 32, :]
-    even = lax.broadcasted_iota(jnp.int32, (32, 128), 1) % 2 == 0
-    for q in range(RANKS):
-        turned = turn_ref[128 * q : 128 * q + 128, :].T
-        out_ref[32 * q : 32 * q + 32, :] = jnp.where(even, turned[:32], turned[32:])
-
-
-def share_kernel(in_ref, out_ref, send_sem, recv_sem):
-    me = lax.axis_index("mode")
-    barrier = pltpu.get_barrier_semaphore()
-
-    def signal(i, carry):
-        pl.semaphore_signal(
-            barrier, inc=1, device_id={"mode": lax.rem(me + i, RANKS)}, device_id_type=MESH)
-        return carry
-
-    lax.fori_loop(1, RANKS, signal, 0)
-    pl.semaphore_wait(barrier, RANKS - 1)
-
-    def copy(i):
-        peer = lax.rem(me + i, RANKS)
-        return pltpu.make_async_remote_copy(
-            src_ref=in_ref.at[pl.ds(pl.multiple_of(32 * peer, 32), 32)],
-            dst_ref=out_ref.at[pl.ds(pl.multiple_of(32 * me, 32), 32)],
-            send_sem=send_sem.at[i],
-            recv_sem=recv_sem.at[i],
-            device_id={"mode": peer},
-            device_id_type=MESH,
-        )
-
-    def start(i, carry):
-        copy(i).start()
-        return carry
-
-    def finish(i, carry):
-        copy(i).wait()
-        return carry
-
-    lax.fori_loop(1, RANKS, start, 0)
-    mine = pl.ds(pl.multiple_of(32 * me, 32), 32)
-    out_ref[mine, :] = in_ref[mine, :]
-    lax.fori_loop(1, RANKS, finish, 0)
+def flat_row(x):
+    return 22 * x if x < 22 else FLAT // 2 + 22 * (x - 22)
 
 
 RESIDUAL = ((1, 44, 45, 0), (21, 22), (1, 0))
 CORRECTION = ((0, 45, 44, 1), (22, 21), (0, 1))
-
-
-def smooth_kernel(
-    lambdas_x, weights, flat_ref, in_x, in_y, out_x, out_y, own_kx, own_my, own_wx, own_ky, mass_ref,
-    lam_ref, out_ref, inward, outward, local, inverse, raw, field, fix, total, side, line, corner,
-    side_in, line_in, corner_in, send_sem, recv_sem):
+TABLES = ("back_high", "back_low", "wave", "twist", "in_x", "in_y", "out_x", "out_y", "own_kx", "own_my", "own_wx",
+          "own_ky", "mass", "lam")
+
+
+def step_kernel(lambdas_x, weights, heights, u_ref, v_ref, lift_ref, *refs):
+    count = len(TABLES)
+    sources, out_ref, refs = refs[:count], refs[count], refs[count + 1 :]
+    held, refs = dict(zip(TABLES, refs[:count], strict=True)), refs[count:]
+    (weak_out, weak_in, modal_out, modal_in, mid_ref, turn_ref, fourier, inward, outward, local, inverse,
+     raw, field, fix, total, side, line, corner, side_in, line_in, corner_in,
+     table_sem, share_send, share_recv, send_sem, recv_sem) = refs
+    me = lax.axis_index("mode")
     ey = lax.axis_index("ey")
     ex = lax.axis_index("ex")
-    left, right = lax.rem(ex + 3, 4), lax.rem(ex + 1, 4)
-    other = 1 - ey
     low_side = ey == 0
-    peers = ({"ex": left}, {"ex": right}, {"ey": other},
-             {"ex": left, "ey": other}, {"ex": right, "ey": other})
+    my_z, my_y, my_c = me // 8, lax.rem(me // 2, 4), lax.rem(me, 2)
+
+    def rank(dz, group):
+        dy, dc = group // 2, lax.rem(group, 2)
+        return 8 * lax.rem(my_z + dz, 4) + 2 * lax.rem(my_y + dy, 4) + lax.rem(my_c + dc, 2)
+
+    def each_rank(act):
+        for dz in (2, 1, 3):
+            act(dz, jnp.int32(0))
+
+        def body(group, carry):
+            for dz in (2, 1, 3, 0):
+                act(dz, group)
+            return carry
+
+        lax.fori_loop(1, 8, body, 0)
+
+    loads = [pltpu.make_async_copy(source, held[name], table_sem.at[at])
+             for at, (name, source) in enumerate(zip(TABLES, sources, strict=True))]
+    for load in loads:
+        load.start()
+
+    left, right, other = lax.rem(ex + 3, 4), lax.rem(ex + 1, 4), 1 - ey
+    peers = ({"ex": left, "ey": other}, {"ex": right, "ey": other}, {"ey": other}, {"ex": left}, {"ex": right})
     barrier = pltpu.get_barrier_semaphore()
+    each_rank(lambda dz, group: pl.semaphore_signal(
+        barrier, inc=1, device_id={"mode": rank(dz, group)}, device_id_type=MESH))
     for peer in peers:
         pl.semaphore_signal(barrier, inc=1, device_id=peer, device_id_type=MESH)
 
-    raw[...] = jnp.zeros((GRID, 128), F32)
-    for x in range(45):
-        raw[LINE * (x + 1) + 1 : LINE * (x + 1) + 23, :] = flat_ref[22 * x : 22 * x + 22, :]
-
+    def advect(half):
+        first = lax.broadcasted_iota(jnp.int32, (FINE_PAD, 128), 1) < 64
+        products = []
+        for f in range(ROWS_DEV):
+            columns = []
+            for e in (2 * half, 2 * half + 1):
+                rows = pl.ds(ROWS_DEV * e + f, NODES * NODES, stride=ROWS_DEV * ELEMS)
+                columns.append(jnp.concatenate([u_ref[rows, :], v_ref[rows, :]], 1))
+            high, low = split(jnp.concatenate(columns, 1))
+            fine = dot(lift_ref[...], jnp.concatenate([high, low, high], 0))
+            half_height = jnp.where(
+                low_side, np.float32(heights[f] / 2.0), np.float32(heights[ROWS_DEV + f] / 2.0))
+            parts = []
+            for e in range(2):
+                block = slice(128 * e, 128 * e + 128)
+                speed = fine[:FINE_PAD, block]
+                turned = pltpu.roll(speed, 64, 1)
+                along = jnp.where(first, speed, turned) * half_height
+                across = jnp.where(first, turned, speed)
+                parts.append(
+                    along * fine[FINE_PAD : 2 * FINE_PAD, block] + across * fine[2 * FINE_PAD :, block])
+            products.append(jnp.concatenate(parts, 1))
+        high, low = split(jnp.concatenate(products, 0))
+        if half == 0:
+            loads[0].wait()
+            loads[1].wait()
+        back_high, back_low = held["back_high"], held["back_low"]
+        weak = dot(back_high[...], high) + dot(back_high[...], low) + dot(back_low[...], high)
+        return jnp.where(low_side, pltpu.roll(weak, OWN - 1, 0), weak)
+
+    def store_weak(half, weak, carried):
+        for e in range(2):
+            for a in range(NODES):
+                x = P_SIZE * (2 * half + e) + a
+                if a == P_SIZE and x < 44:
+                    continue
+                value = weak[LINE * a : LINE * a + 22, 128 * e : 128 * e + 128]
+                if a == 0 and e == 1:
+                    value += weak[LINE * P_SIZE : LINE * P_SIZE + 22, :128]
+                if a == 0 and e == 0 and half == 1:
+                    value += carried
+                weak_out[flat_row(x) : flat_row(x) + 22, :] = value
+        spare = (484, 512) if half == 0 else (1018, 1024)
+        weak_out[spare[0] : spare[1], :] = jnp.zeros((spare[1] - spare[0], 128), F32)
+        return weak[LINE * P_SIZE : LINE * P_SIZE + 22, 128:]
+
+    def share(stage, half):
+        source, target = ((weak_out, weak_in), (modal_out, modal_in))[stage]
+        base, number = FLAT // 2 * half, 2 * stage + half
+
+        def copy(dz, group):
+            at = 8 * dz + group
+            peer = rank(dz, group)
+            return pltpu.make_async_remote_copy(
+                src_ref=source.at[pl.ds(pl.multiple_of(base + 16 * peer, 16), 16)],
+                dst_ref=target.at[pl.ds(pl.multiple_of(base + 16 * me, 16), 16)],
+                send_sem=share_send.at[number, at],
+                recv_sem=share_recv.at[number, at],
+                device_id={"mode": peer},
+                device_id_type=MESH,
+            )
+
+        return copy
+
+    def send(stage, half):
+        copy = share(stage, half)
+        each_rank(lambda dz, group: copy(dz, group).start())
+        source, target = ((weak_out, weak_in), (modal_out, modal_in))[stage]
+        mine = pl.ds(pl.multiple_of(FLAT // 2 * half + 16 * me, 16), 16)
+        target[mine, :] = source[mine, :]
+
+    def receive(stage, half):
+        copy = share(stage, half)
+        each_rank(lambda dz, group: copy(dz, group).wait_recv())
+
+    def transform(half):
+        base = FLAT // 2 * half
+        for block in range(2):
+            rows = slice(8 * block, 8 * block + 8)
+            starts = [base + 16 * d + 8 * block for d in range(RANKS)]
+            found = real_transform([weak_in[s : s + 8, :] for s in starts])
+            for r in range(1, 16):
+                mid_ref[2 * r, rows, :], mid_ref[2 * r + 1, rows, :] = found[r]
+            mid_ref[0, rows, :] = found[0][0]
+            mid_ref[1, rows, :] = found[16][0]
+        first = lax.broadcasted_iota(jnp.int32, (16, 128), 1) < 64
+        for rp in range(16):
+            real, imag = mid_ref[2 * rp], mid_ref[2 * rp + 1]
+            both = jnp.concatenate(
+                [jnp.where(first, real, pltpu.roll(imag, 64, 1)),
+                 jnp.where(first, pltpu.roll(real, 64, 1), imag)], 0)
+            high, low = split(both)
+            table = fourier[rp]
+            found = dot_rows(table, jnp.concatenate([high, high], 1)) + dot_rows(table[:, :128], low)
+            for at in range(2):
+                r = rp if at == 0 else (32 - rp if rp else 16)
+                for c in range(2):
+                    start = 32 * (2 * at + c)
+                    for k in range(2):
+                        turn_ref[pl.ds(4 * r + 2 * c + k, 32, stride=128), :] = found[start : start + 32, :]
+        even = lax.broadcasted_iota(jnp.int32, (16, 128), 1) % 2 == 0
+        for q in range(RANKS):
+            turned = turn_ref[128 * q : 128 * q + 128, :].T
+            modal_out[base + 16 * q : base + 16 * q + 16, :] = jnp.where(even, turned[:16], turned[16:])
+
+    carried = store_weak(0, advect(0), None)
+    pl.semaphore_wait(barrier, RANKS - 1 + 5)
+    send(0, 0)
+    store_weak(1, advect(1), carried)
+    send(0, 1)
+
+    for load in loads[2:]:
+        load.wait()
+    for rp in range(16):
+        for at in range(4):
+            pair = held["twist"][rp, 2 * at : 2 * at + 2, :]
+            high, low = split(held["wave"][0] * pair[:1] + held["wave"][1] * pair[1:])
+            fourier[rp, 32 * at : 32 * at + 32, :128] = high
+            fourier[rp, 32 * at : 32 * at + 32, 128:] = low
     lane = lax.broadcasted_iota(jnp.int32, (1, 128), 1)
-    mode = (lax.axis_index("mode") * 32 + lane // 4).astype(F32)
+    mode = (me * 32 + lane // 4).astype(F32)
     shift = shift_base + (np.float32(span_rate) * mode) ** 2
     for f in range(ROWS_DEV):
         for i in range(EXT_POINTS):
             row = 16 * (EXT_POINTS * f + i)
-            high, low = split(in_x[i : i + 1, :] * in_y[ey, f])
+            high, low = split(held["in_x"][i : i + 1, :] * held["in_y"][ey, f])
             inward[0, row : row + 16, :] = high
             inward[1, row : row + 16, :] = low
-            inverse[row : row + 16, :] = 1.0 / (lam_ref[ey, f] + (shift + np.float32(lambdas_x[i])))
-    high, low = split(jnp.concatenate([out_x[a : a + 1, :] * out_y[ey] for a in range(EXT_POINTS)], 0))
+            inverse[row : row + 16, :] = 1.0 / (held["lam"][ey, f] + (shift + np.float32(lambdas_x[i])))
+    high, low = split(jnp.concatenate(
+        [held["out_x"][a : a + 1, :] * held["out_y"][ey] for a in range(EXT_POINTS)], 0))
     outward[0], outward[1] = high, low
     high, low = split(jnp.concatenate(
-        [own_kx[a : a + 1, :] * own_my[ey] + own_wx[a : a + 1, :] * own_ky[ey] for a in range(NODES)], 0))
+        [held["own_kx"][a : a + 1, :] * held["own_my"][ey] + held["own_wx"][a : a + 1, :] * held["own_ky"][ey]
+         for a in range(NODES)], 0))
     local[0], local[1] = high, low
-
-    pl.semaphore_wait(barrier, 5)
+    raw[...] = jnp.zeros((GRID, 128), F32)
+
+    for half in range(2):
+        receive(0, half)
+        transform(half)
+        send(1, half)
+    for half in range(2):
+        receive(1, half)
+        for x in range(22 * half, 22 + 23 * half):
+            raw[LINE * (x + 1) + 1 : LINE * (x + 1) + 23, :] = modal_in[flat_row(x) : flat_row(x) + 22, :]
 
     def exchange(number, grid, kind):
         (to_left, to_right, from_right, from_left), lower, upper = kind
-        side[number, 0] = grid[LINE * to_left : LINE * to_left + 48, :]
-        side[number, 1] = grid[LINE * to_right : LINE * to_right + 48, :]
         zero = jnp.zeros((4, 128), F32)
         pieces = []
         for step in range(2):
@@ -468,22 +518,27 @@
             pieces.append(rows)
         for at, column in enumerate((to_left, to_right)):
             corner[number, at] = jnp.concatenate([p[column : column + 2] for p in pieces] + [zero], 0)
+        side[number, 0] = grid[LINE * to_left : LINE * to_left + 48, :]
+        side[number, 1] = grid[LINE * to_right : LINE * to_right + 48, :]
         sends = (
+            (corner.at[number, 0], corner_in.at[number, 0]),
+            (corner.at[number, 1], corner_in.at[number, 1]),
+            (line.at[number], line_in.at[number]),
             (side.at[number, 0], side_in.at[number, 0]),
-            (side.at[number, 1], side_in.at[number, 1]),
-            (line.at[number], line_in.at[number]),
-            (corner.at[number, 0], corner_in.at[number, 0]),
-            (corner.at[number, 1], corner_in.at[number, 1]))
+            (side.at[number, 1], side_in.at[number, 1]))
         copies = []
         for at, ((source, target), peer) in enumerate(zip(sends, peers, strict=True)):
             copies.append(pltpu.make_async_remote_copy(
                 src_ref=source, dst_ref=target, send_sem=send_sem.at[number, at],
                 recv_sem=recv_sem.at[number, at], device_id=peer, device_id_type=MESH))
             copies[-1].start()
-        for sent in copies:
-            sent.wait()
+        copies[3].wait_recv()
+        copies[4].wait_recv()
         grid[LINE * from_right : LINE * from_right + 48, :] += side_in[number, 0]
         grid[LINE * from_left : LINE * from_left + 48, :] += side_in[number, 1]
+        copies[2].wait_recv()
+        copies[0].wait_recv()
+        copies[1].wait_recv()
         zeros = jnp.zeros((COLS, 128), F32)
         for step in range(2):
             rows = [line_in[number, step]]
@@ -497,6 +552,7 @@
             where_up = pl.ds(upper[1] + step, COLS, stride=LINE)
             grid[where_low, :] += jnp.where(low_side, added, zeros)
             grid[where_up, :] += jnp.where(low_side, zeros, added)
+        return copies
 
     def solve(source, target):
         value = jnp.concatenate(
@@ -510,73 +566,60 @@
         for e in range(ELEMS):
             target[264 * e : 264 * e + WINDOW, :] += back[:, 128 * e : 128 * e + 128]
 
+    sent = []
     field[...] = raw[...]
-    exchange(0, field, RESIDUAL)
+    sent += exchange(0, field, RESIDUAL)
     solve(field, total)
-    exchange(1, total, CORRECTION)
+    sent += exchange(1, total, CORRECTION)
     value = jnp.concatenate(
         [total[264 * e + LINE : 264 * e + LINE + OWN, :] for e in range(ELEMS)], 1)
     high, low = split(value)
     applied = dot(local[0], high) + dot(local[0], low) + dot(local[1], high)
     coefficient = jnp.concatenate(
-        [(np.float32(weights[a] * element_width / 2.0) * shift) * mass_ref[ey] for a in range(NODES)], 0)
+        [(np.float32(weights[a] * element_width / 2.0) * shift) * held["mass"][ey] for a in range(NODES)], 0)
     applied = applied + value * jnp.concatenate([coefficient] * ELEMS, 1)
     field[...] = raw[...]
     for e in range(ELEMS):
         field[264 * e + LINE : 264 * e + LINE + OWN, :] -= applied[:, 128 * e : 128 * e + 128]
-    exchange(2, field, RESIDUAL)
+    sent += exchange(2, field, RESIDUAL)
     solve(field, fix)
-    exchange(3, fix, CORRECTION)
-    total[...] += fix[...]
+    sent += exchange(3, fix, CORRECTION)
+    out_ref[...] = total[...] + fix[...]
+    for one in sent:
+        one.wait_send()
+    for stage in range(2):
+        for half in range(2):
+            copy = share(stage, half)
+            each_rank(lambda dz, group, copy=copy: copy(dz, group).wait_send())
+
+
+def place_kernel(grid_ref, out_ref):
+    low_side = lax.axis_index("ey") == 0
     for e in range(ELEMS):
         for f in range(ROWS_DEV):
             for a in range(NODES):
                 start = LINE * (P_SIZE * e + 1 + a) + P_SIZE * f
                 out_ref[pl.ds(96 * a + 2 * e + f, NODES, stride=8), :] = jnp.where(
-                    low_side, total[start : start + NODES, :], total[start + 1 : start + 1 + NODES, :])
+                    low_side, grid_ref[start : start + NODES, :], grid_ref[start + 1 : start + 1 + NODES, :])
 
 
 def on_device(stream_speed, normal_speed):
     single, lambdas_x, weights, heights = all_tables()
     vmem = pl.BlockSpec(memory_space=pltpu.VMEM)
-    flat = jax.ShapeDtypeStruct((FLAT, 128), F32)
-
-    def share(value, number):
-        return pl.pallas_call(
-            share_kernel,
-            out_shape=flat,
-            in_specs=[vmem],
-            out_specs=vmem,
-            scratch_shapes=[pltpu.SemaphoreType.DMA((RANKS,)), pltpu.SemaphoreType.DMA((RANKS,))],
-            compiler_params=pltpu.CompilerParams(collective_id=number, has_side_effects=True),
-            name=f"share_{number}",
-        )(value)
-
+    anywhere = pl.BlockSpec(memory_space=pl.ANY)
     tables = {name: jnp.asarray(table) for name, table in single.items()}
-    weak = pl.pallas_call(
-        functools.partial(advect_kernel, heights),
-        out_shape=flat,
-        in_specs=[vmem] * 5,
+    grid = pltpu.VMEM((GRID, 128), F32)
+    flat = pltpu.VMEM((FLAT, 128), F32)
+    solved = pl.pallas_call(
+        functools.partial(step_kernel, lambdas_x, weights, heights),
+        out_shape=jax.ShapeDtypeStruct((GRID, 128), F32),
+        in_specs=[vmem] * 3 + [anywhere] * len(TABLES),
         out_specs=vmem,
-        name="advect",
-    )(stream_speed.reshape(1152, 64), normal_speed.reshape(1152, 64), tables["lift"],
-      tables["back_high"], tables["back_low"])
-    spectra = pl.pallas_call(
-        transform_kernel,
-        out_shape=flat,
-        in_specs=[vmem] * 2,
-        out_specs=vmem,
-        scratch_shapes=[pltpu.VMEM((32, 32, 128), F32), pltpu.VMEM((4096, 64), F32)],
-        name="transform",
-    )(share(weak, 1), tables["fourier"])
-    names = ("in_x", "in_y", "out_x", "out_y", "own_kx", "own_my", "own_wx", "own_ky", "mass", "lam")
-    grid = pltpu.VMEM((GRID, 128), F32)
-    solved = pl.pallas_call(
-        functools.partial(smooth_kernel, lambdas_x, weights),
-        out_shape=jax.ShapeDtypeStruct((1152, 128), F32),
-        in_specs=[vmem] * (1 + len(names)),
-        out_specs=vmem,
-        scratch_shapes=[
+        scratch_shapes=[pltpu.VMEM(single[name].shape, single[name].dtype) for name in TABLES] + [
+            flat, flat, flat, flat,
+            pltpu.VMEM((32, 16, 128), F32),
+            pltpu.VMEM((4096, 32), F32),
+            pltpu.VMEM((16, 128, 256), BF16),
             pltpu.VMEM((2, SPECTRAL, WINDOW), BF16),
             pltpu.VMEM((2, WINDOW, SPECTRAL), BF16),
             pltpu.VMEM((2, OWN, OWN), BF16),
@@ -588,13 +631,24 @@
             pltpu.VMEM((4, 2, 48, 128), F32),
             pltpu.VMEM((4, 2, COLS, 128), F32),
             pltpu.VMEM((4, 2, 8, 128), F32),
+            pltpu.SemaphoreType.DMA((len(TABLES),)),
+            pltpu.SemaphoreType.DMA((4, 32)),
+            pltpu.SemaphoreType.DMA((4, 32)),
             pltpu.SemaphoreType.DMA((4, 5)),
             pltpu.SemaphoreType.DMA((4, 5)),
         ],
-        compiler_params=pltpu.CompilerParams(collective_id=3, has_side_effects=True),
-        name="smooth",
-    )(share(spectra, 2), *[tables[name] for name in names])
-    return solved.reshape(12, 12, 4, 2, 128)
+        compiler_params=pltpu.CompilerParams(collective_id=1, has_side_effects=True),
+        name="step",
+    )(stream_speed.reshape(1152, 64), normal_speed.reshape(1152, 64), tables["lift"],
+      *[tables[name] for name in TABLES])
+    placed = pl.pallas_call(
+        place_kernel,
+        out_shape=jax.ShapeDtypeStruct((1152, 128), F32),
+        in_specs=[vmem],
+        out_specs=vmem,
+        name="place",
+    )(solved)
+    return placed.reshape(12, 12, 4, 2, 128)
 
 
 def solution(mesh):

time: 87 us -> 64.9 us (0.75)
  the two profiles are of different devices: /device:TPU:24 before, /device:TPU:8 now
where the time goes in v1:
time: 64.9 us; the launch traced here: 64.5 us
  Pallas kernels  64.5 us (99%)
    pallas_call x1, Pallas kernels, on_device(): pl.pallas_call(functools.partial(step_kernel, lambdas_x, weights, heights...  62.5 us
    pallas_call x1, Pallas kernels, on_device(): pl.pallas_call(place_kernel, out_shape=jax.ShapeDtypeStruct((1152, 128),...  2.05 us

profile of v1, /device:TPU:8, one launch (start us, length us, event | category | flops | bytes accessed | tf_op | source)
XLA Modules:
  0.0 64.5 jit_solution(15530589609010278530)
XLA Ops:
  0.0 62.5 %step.1.grid_ref = f32[1152,128]{1,0:T(8,128)} custom-call(f32[1152,64]{1,0:T(8,128)} %bitcast.3, f32[1152,64]{1,0:T(8,128)} %bitcast.4, bf16[1008,432]{1,0:T(8,128)(2,1)} %constant.30.clone.lift_ref, bf16[288,672]{1,0:T(8,128)(2,1)} %constant.31.clone.refs_0_, bf16[288,672]{1,0:T(8,128)(2,1)} %constant.32.clone.refs_1_, ...), custom_call_target="tpu_custom_call" | custom-call | tf_op jit(solution)/shard_map/step/pallas_call | solution.py:613
  62.5 2.0 %place.1 = f32[1152,128]{1,0:T(8,128)} custom-call(f32[1152,128]{1,0:T(8,128)} %step.1.grid_ref), custom_call_target="tpu_custom_call" | custom-call | tf_op jit(solution)/shard_map/place/pallas_call | solution.py:644

commit v2 on v1

--- a/solution.py
+++ b/solution.py
@@ -23,8 +23,6 @@
 GRID = COLS * LINE
 FLAT = 1024
 EXT_POINTS = NODES + 2
-SPECTRAL = ROWS_DEV * EXT_POINTS * 16
-WINDOW = EXT_POINTS * LINE
 OWN = NODES * LINE
 
 MESH = pl.DeviceIdType.MESH
@@ -201,12 +199,13 @@
     lift = lift.reshape(3 * FINE_PAD, nodes)
     lift_high, lift_low = bf16_pair(lift)
     lift_cat = np.concatenate([lift_high, lift_high, lift_low], 1)
-    back = np.zeros((NODES, LINE, ROWS_DEV, FINE_PAD))
+    back = np.zeros((ROWS_DEV, NODES, 16, FINE_PAD))
     quad = np.kron(gauss_weights, gauss_weights)
     back_one = -(np.kron(interp.T, interp.T) * quad[None, :]).reshape(NODES, NODES, fine)
     for f in range(ROWS_DEV):
-        back[:, P_SIZE * f : P_SIZE * f + NODES, f, :fine] += back_one
-    back_high, back_low = bf16_pair(back.reshape(NODES * LINE, ROWS_DEV * FINE_PAD))
+        back[f, :, 3 * f : 3 * f + NODES, :fine] = back_one
+    back_high, back_low = bf16_pair(back.reshape(ROWS_DEV, NODES * 16, FINE_PAD))
+    back_cat = np.concatenate([back_high, back_high, back_low], 2)
     plane = np.arange(64)[None, :]
     angle = 2.0 * np.pi * ((np.arange(32)[:, None] * plane) % 64) / 64.0
     wave = np.tile(np.stack([np.cos(angle), np.sin(angle)]), (1, 1, 2))
@@ -227,14 +226,15 @@
                 twist[rp, 2 * half + 1, :, 0] = -sine
                 twist[rp, 2 * half + 1, :, 1] = sign * cosine
     twist = twist.reshape(16, 8, 128)
-    line_basis = np.zeros((2, ROWS_DEV, LINE, 16))
+    line_basis = np.zeros((2, ROWS_DEV, 16, 16))
     line_lambda = np.ones((2, ROWS_DEV, 16))
     line_mass = np.zeros((2, LINE))
-    line_stiff = np.zeros((2, LINE, LINE))
+    row_mass = np.zeros((2, ROWS_DEV, 16))
+    row_stiff = np.zeros((2, ROWS_DEV, 16, 16))
     top = P_SIZE * ROWS_TOTAL
     for ey in range(2):
-        low = 21 * ey
         for f in range(ROWS_DEV):
+            low = 21 * ey + 8 * f
             row = ROWS_DEV * ey + f
             line_lambda[ey, f, :EXT_POINTS] = lambdas_y[row]
             for b in range(EXT_POINTS):
@@ -244,24 +244,23 @@
             for b in range(NODES):
                 g = P_SIZE * row + b
                 if 0 < g < top:
-                    line_mass[ey, g - low] += heights[row] / 2.0 * weights[b]
+                    line_mass[ey, g - 21 * ey] += heights[row] / 2.0 * weights[b]
+                    row_mass[ey, f, g - low] = heights[row] / 2.0 * weights[b]
                     for c in range(NODES):
                         h = P_SIZE * row + c
                         if 0 < h < top:
-                            line_stiff[ey, g - low, h - low] += 2.0 / heights[row] * stiffness[b, c]
-    ones_line = np.ones(LINE)
-    in_x = np.kron(basis_x.T, ones_line[None, :])
+                            row_stiff[ey, f, g - low, h - low] = 2.0 / heights[row] * stiffness[b, c]
+    ones_line = np.ones((1, 16))
+    in_x = np.kron(basis_x.T, ones_line)
     in_y = np.tile(np.transpose(line_basis, (0, 1, 3, 2)), (1, 1, 1, EXT_POINTS))
-    out_x = np.tile(np.kron(basis_x, np.ones((1, 16))), (1, ROWS_DEV))
-    out_y = np.concatenate(
-        [np.tile(line_basis[:, f], (1, 1, EXT_POINTS)) for f in range(ROWS_DEV)], 2)
-    eye = np.eye(NODES)
-    own_kx = np.kron(stiffness * (2.0 / element_width), ones_line[None, :])
-    own_my = np.tile(line_mass[:, :, None] * np.eye(LINE)[None], (1, 1, NODES))
-    own_wx = np.kron(np.diag(weights) * (element_width / 2.0), ones_line[None, :])
-    own_ky = np.tile(line_stiff, (1, 1, NODES))
+    out_x = np.kron(basis_x, ones_line)
+    out_y = np.tile(line_basis, (1, 1, 1, EXT_POINTS))
+    own_kx = np.kron(stiffness * (2.0 / element_width), ones_line)
+    own_my = np.tile(row_mass[..., None] * np.eye(16), (1, 1, 1, NODES))
+    own_wx = np.kron(np.diag(weights) * (element_width / 2.0), ones_line)
+    own_ky = np.tile(row_stiff, (1, 1, 1, NODES))
     wide = np.ones((1, 1, 128))
-    single = dict(lift=lift_cat, back_high=back_high, back_low=back_low)
+    single = dict(lift=lift_cat, back=back_cat)
     single.update({name: np.asarray(table, np.float32) for name, table in dict(
         wave=wave, twist=twist,
         in_x=in_x, in_y=in_y, out_x=out_x, out_y=out_y,
@@ -313,11 +312,11 @@
 
 RESIDUAL = ((1, 44, 45, 0), (21, 22), (1, 0))
 CORRECTION = ((0, 45, 44, 1), (22, 21), (0, 1))
-TABLES = ("back_high", "back_low", "wave", "twist", "in_x", "in_y", "out_x", "out_y", "own_kx", "own_my", "own_wx",
+TABLES = ("stream", "normal", "lift", "back", "wave", "twist", "in_x", "in_y", "out_x", "out_y", "own_kx", "own_my", "own_wx",
           "own_ky", "mass", "lam")
 
 
-def step_kernel(lambdas_x, weights, heights, u_ref, v_ref, lift_ref, *refs):
+def step_kernel(lambdas_x, weights, heights, *refs):
     count = len(TABLES)
     sources, out_ref, refs = refs[:count], refs[count], refs[count + 1 :]
     held, refs = dict(zip(TABLES, refs[:count], strict=True)), refs[count:]
@@ -335,20 +334,24 @@
         return 8 * lax.rem(my_z + dz, 4) + 2 * lax.rem(my_y + dy, 4) + lax.rem(my_c + dc, 2)
 
     def each_rank(act):
-        for dz in (2, 1, 3):
-            act(dz, jnp.int32(0))
-
-        def body(group, carry):
-            for dz in (2, 1, 3, 0):
-                act(dz, group)
+        def apart(i, carry):
+            for dz in (2, 1, 3):
+                act(dz, lax.rem(i + 4, 8))
             return carry
 
-        lax.fori_loop(1, 8, body, 0)
+        def beside(i, carry):
+            act(0, i)
+            return carry
+
+        lax.fori_loop(0, 8, apart, 0)
+        lax.fori_loop(4, 8, beside, 0)
+        lax.fori_loop(1, 4, beside, 0)
 
     loads = [pltpu.make_async_copy(source, held[name], table_sem.at[at])
              for at, (name, source) in enumerate(zip(TABLES, sources, strict=True))]
-    for load in loads:
+    for load in loads[:3]:
         load.start()
+    u_ref, v_ref, lift_ref = held["stream"], held["normal"], held["lift"]
 
     left, right, other = lax.rem(ex + 3, 4), lax.rem(ex + 1, 4), 1 - ey
     peers = ({"ex": left, "ey": other}, {"ex": right, "ey": other}, {"ey": other}, {"ex": left}, {"ex": right})
@@ -357,35 +360,43 @@
         barrier, inc=1, device_id={"mode": rank(dz, group)}, device_id_type=MESH))
     for peer in peers:
         pl.semaphore_signal(barrier, inc=1, device_id=peer, device_id_type=MESH)
+    for load in loads[3:]:
+        load.start()
+    for load in loads[:3]:
+        load.wait()
 
     def advect(half):
         first = lax.broadcasted_iota(jnp.int32, (FINE_PAD, 128), 1) < 64
-        products = []
+        columns = []
         for f in range(ROWS_DEV):
-            columns = []
             for e in (2 * half, 2 * half + 1):
                 rows = pl.ds(ROWS_DEV * e + f, NODES * NODES, stride=ROWS_DEV * ELEMS)
                 columns.append(jnp.concatenate([u_ref[rows, :], v_ref[rows, :]], 1))
-            high, low = split(jnp.concatenate(columns, 1))
-            fine = dot(lift_ref[...], jnp.concatenate([high, low, high], 0))
+        high, low = split(jnp.concatenate(columns, 1))
+        fine = dot(lift_ref[...], jnp.concatenate([high, low, high], 0))
+        weak = []
+        for f in range(ROWS_DEV):
             half_height = jnp.where(
                 low_side, np.float32(heights[f] / 2.0), np.float32(heights[ROWS_DEV + f] / 2.0))
             parts = []
             for e in range(2):
-                block = slice(128 * e, 128 * e + 128)
+                start = 256 * f + 128 * e
+                block = slice(start, start + 128)
                 speed = fine[:FINE_PAD, block]
                 turned = pltpu.roll(speed, 64, 1)
                 along = jnp.where(first, speed, turned) * half_height
                 across = jnp.where(first, turned, speed)
                 parts.append(
                     along * fine[FINE_PAD : 2 * FINE_PAD, block] + across * fine[2 * FINE_PAD :, block])
-            products.append(jnp.concatenate(parts, 1))
-        high, low = split(jnp.concatenate(products, 0))
-        if half == 0:
-            loads[0].wait()
-            loads[1].wait()
-        back_high, back_low = held["back_high"], held["back_low"]
-        weak = dot(back_high[...], high) + dot(back_high[...], low) + dot(back_low[...], high)
+            high, low = split(jnp.concatenate(parts, 1))
+            if half == 0 and f == 0:
+                loads[3].wait()
+            weak.append(dot(held["back"][f], jnp.concatenate([high, low, high], 0)))
+        lines = []
+        for a in range(NODES):
+            low_row, high_row = slice(16 * a, 16 * a + 8), slice(16 * a + 8, 16 * a + 16)
+            lines += [weak[0][low_row], weak[0][high_row] + weak[1][low_row], weak[1][high_row]]
+        weak = jnp.concatenate(lines, 0)
         return jnp.where(low_side, pltpu.roll(weak, OWN - 1, 0), weak)
 
     def store_weak(half, weak, carried):
@@ -404,34 +415,31 @@
         weak_out[spare[0] : spare[1], :] = jnp.zeros((spare[1] - spare[0], 128), F32)
         return weak[LINE * P_SIZE : LINE * P_SIZE + 22, 128:]
 
-    def share(stage, half):
+    def send(stage, half):
         source, target = ((weak_out, weak_in), (modal_out, modal_in))[stage]
         base, number = FLAT // 2 * half, 2 * stage + half
-
-        def copy(dz, group):
-            at = 8 * dz + group
+        mine = pl.ds(pl.multiple_of(base + 16 * me, 16), 16)
+
+        def start(dz, group):
             peer = rank(dz, group)
-            return pltpu.make_async_remote_copy(
+            pltpu.make_async_remote_copy(
                 src_ref=source.at[pl.ds(pl.multiple_of(base + 16 * peer, 16), 16)],
-                dst_ref=target.at[pl.ds(pl.multiple_of(base + 16 * me, 16), 16)],
-                send_sem=share_send.at[number, at],
-                recv_sem=share_recv.at[number, at],
+                dst_ref=target.at[mine],
+                send_sem=share_send.at[number],
+                recv_sem=share_recv.at[number],
                 device_id={"mode": peer},
                 device_id_type=MESH,
-            )
-
-        return copy
-
-    def send(stage, half):
-        copy = share(stage, half)
-        each_rank(lambda dz, group: copy(dz, group).start())
+            ).start()
+
+        each_rank(start)
+        target[mine, :] = source[mine, :]
+
+    def bytes_of(stage, half):
         source, target = ((weak_out, weak_in), (modal_out, modal_in))[stage]
-        mine = pl.ds(pl.multiple_of(FLAT // 2 * half + 16 * me, 16), 16)
-        target[mine, :] = source[mine, :]
-
-    def receive(stage, half):
-        copy = share(stage, half)
-        each_rank(lambda dz, group: copy(dz, group).wait_recv())
+        rows, number = pl.ds(0, 16 * (RANKS - 1)), 2 * stage + half
+        return pltpu.make_async_remote_copy(
+            src_ref=source.at[rows], dst_ref=target.at[rows], send_sem=share_send.at[number],
+            recv_sem=share_recv.at[number], device_id={"mode": rank(2, 0)}, device_id_type=MESH)
 
     def transform(half):
         base = FLAT // 2 * half
@@ -464,12 +472,12 @@
             modal_out[base + 16 * q : base + 16 * q + 16, :] = jnp.where(even, turned[:16], turned[16:])
 
     carried = store_weak(0, advect(0), None)
+    store_weak(1, advect(1), carried)
     pl.semaphore_wait(barrier, RANKS - 1 + 5)
     send(0, 0)
-    store_weak(1, advect(1), carried)
     send(0, 1)
 
-    for load in loads[2:]:
+    for load in loads[4:]:
         load.wait()
     for rp in range(16):
         for at in range(4):
@@ -482,28 +490,34 @@
     shift = shift_base + (np.float32(span_rate) * mode) ** 2
     for f in range(ROWS_DEV):
         for i in range(EXT_POINTS):
-            row = 16 * (EXT_POINTS * f + i)
+            rows = slice(16 * i, 16 * i + 16)
             high, low = split(held["in_x"][i : i + 1, :] * held["in_y"][ey, f])
-            inward[0, row : row + 16, :] = high
-            inward[1, row : row + 16, :] = low
-            inverse[row : row + 16, :] = 1.0 / (held["lam"][ey, f] + (shift + np.float32(lambdas_x[i])))
-    high, low = split(jnp.concatenate(
-        [held["out_x"][a : a + 1, :] * held["out_y"][ey] for a in range(EXT_POINTS)], 0))
-    outward[0], outward[1] = high, low
-    high, low = split(jnp.concatenate(
-        [held["own_kx"][a : a + 1, :] * held["own_my"][ey] + held["own_wx"][a : a + 1, :] * held["own_ky"][ey]
-         for a in range(NODES)], 0))
-    local[0], local[1] = high, low
+            inward[f, 0, rows, :], inward[f, 1, rows, :] = high, low
+            high, low = split(held["out_x"][i : i + 1, :] * held["out_y"][ey, f])
+            outward[f, 0, rows, :], outward[f, 1, rows, :] = high, low
+            inverse[f, rows, :] = 1.0 / (held["lam"][ey, f] + (shift + np.float32(lambdas_x[i])))
+        for a in range(NODES):
+            rows = slice(16 * a, 16 * a + 16)
+            high, low = split(
+                held["own_kx"][a : a + 1, :] * held["own_my"][ey, f]
+                + held["own_wx"][a : a + 1, :] * held["own_ky"][ey, f])
+            local[f, 0, rows, :], local[f, 1, rows, :] = high, low
+    mass_shift = [held["mass"][ey, 8 * g : 8 * g + 8, :] * shift for g in range(3)]
     raw[...] = jnp.zeros((GRID, 128), F32)
 
     for half in range(2):
-        receive(0, half)
+        bytes_of(0, half).wait_recv()
         transform(half)
         send(1, half)
     for half in range(2):
-        receive(1, half)
+        bytes_of(1, half).wait_recv()
         for x in range(22 * half, 22 + 23 * half):
             raw[LINE * (x + 1) + 1 : LINE * (x + 1) + 23, :] = modal_in[flat_row(x) : flat_row(x) + 22, :]
+
+    def all_of(number, rows, at):
+        return pltpu.make_async_remote_copy(
+            src_ref=raw.at[pl.ds(0, rows)], dst_ref=raw.at[pl.ds(0, rows)], send_sem=send_sem.at[number],
+            recv_sem=recv_sem.at[number, at], device_id=peers[2], device_id_type=MESH)
 
     def exchange(number, grid, kind):
         (to_left, to_right, from_right, from_left), lower, upper = kind
@@ -526,19 +540,14 @@
             (line.at[number], line_in.at[number]),
             (side.at[number, 0], side_in.at[number, 0]),
             (side.at[number, 1], side_in.at[number, 1]))
-        copies = []
         for at, ((source, target), peer) in enumerate(zip(sends, peers, strict=True)):
-            copies.append(pltpu.make_async_remote_copy(
-                src_ref=source, dst_ref=target, send_sem=send_sem.at[number, at],
-                recv_sem=recv_sem.at[number, at], device_id=peer, device_id_type=MESH))
-            copies[-1].start()
-        copies[3].wait_recv()
-        copies[4].wait_recv()
+            pltpu.make_async_remote_copy(
+                src_ref=source, dst_ref=target, send_sem=send_sem.at[number],
+                recv_sem=recv_sem.at[number, at // 3], device_id=peer, device_id_type=MESH).start()
+        all_of(number, 96, 1).wait_recv()
         grid[LINE * from_right : LINE * from_right + 48, :] += side_in[number, 0]
         grid[LINE * from_left : LINE * from_left + 48, :] += side_in[number, 1]
-        copies[2].wait_recv()
-        copies[0].wait_recv()
-        copies[1].wait_recv()
+        all_of(number, 112, 0).wait_recv()
         zeros = jnp.zeros((COLS, 128), F32)
         for step in range(2):
             rows = [line_in[number, step]]
@@ -552,45 +561,66 @@
             where_up = pl.ds(upper[1] + step, COLS, stride=LINE)
             grid[where_low, :] += jnp.where(low_side, added, zeros)
             grid[where_up, :] += jnp.where(low_side, zeros, added)
-        return copies
+
+    def rows_of(source, f, first, count):
+        return jnp.concatenate(
+            [jnp.concatenate(
+                [source[264 * e + LINE * (first + a) + 8 * f : 264 * e + LINE * (first + a) + 8 * f + 16, :]
+                 for a in range(count)], 0) for e in range(ELEMS)], 1)
+
+    def apply(matrix, value):
+        high, low = split(value)
+        return dot(matrix[0], high) + dot(matrix[0], low) + dot(matrix[1], high)
+
+    def gathered(parts, x, g, first, count):
+        found = None
+        for e in range(ELEMS):
+            a = x - P_SIZE * e - first
+            if not 0 <= a < count:
+                continue
+            for f in range(ROWS_DEV):
+                if 0 <= g - f < 2:
+                    row = 16 * a + 8 * (g - f)
+                    term = parts[f][row : row + 8, 128 * e : 128 * e + 128]
+                    found = term if found is None else found + term
+        return found
 
     def solve(source, target):
-        value = jnp.concatenate(
-            [source[264 * e : 264 * e + WINDOW, :] for e in range(ELEMS)], 1)
-        high, low = split(value)
-        modal = dot(inward[0], high) + dot(inward[0], low) + dot(inward[1], high)
-        modal = modal * jnp.concatenate([inverse[...]] * ELEMS, 1)
-        high, low = split(modal)
-        back = dot(outward[0], high) + dot(outward[0], low) + dot(outward[1], high)
-        target[...] = jnp.zeros((GRID, 128), F32)
-        for e in range(ELEMS):
-            target[264 * e : 264 * e + WINDOW, :] += back[:, 128 * e : 128 * e + 128]
-
-    sent = []
+        parts = []
+        for f in range(ROWS_DEV):
+            modal = apply(inward.at[f], rows_of(source, f, 0, EXT_POINTS))
+            parts.append(apply(outward.at[f], modal * jnp.concatenate([inverse[f]] * ELEMS, 1)))
+        for x in range(COLS):
+            for g in range(3):
+                found = gathered(parts, x, g, 0, EXT_POINTS)
+                row = LINE * x + 8 * g
+                target[row : row + 8, :] = jnp.zeros((8, 128), F32) if found is None else found
+
     field[...] = raw[...]
-    sent += exchange(0, field, RESIDUAL)
+    exchange(0, field, RESIDUAL)
     solve(field, total)
-    sent += exchange(1, total, CORRECTION)
-    value = jnp.concatenate(
-        [total[264 * e + LINE : 264 * e + LINE + OWN, :] for e in range(ELEMS)], 1)
-    high, low = split(value)
-    applied = dot(local[0], high) + dot(local[0], low) + dot(local[1], high)
-    coefficient = jnp.concatenate(
-        [(np.float32(weights[a] * element_width / 2.0) * shift) * held["mass"][ey] for a in range(NODES)], 0)
-    applied = applied + value * jnp.concatenate([coefficient] * ELEMS, 1)
-    field[...] = raw[...]
-    for e in range(ELEMS):
-        field[264 * e + LINE : 264 * e + LINE + OWN, :] -= applied[:, 128 * e : 128 * e + 128]
-    sent += exchange(2, field, RESIDUAL)
+    exchange(1, total, CORRECTION)
+    parts = [apply(local.at[f], rows_of(total, f, 1, NODES)) for f in range(ROWS_DEV)]
+    for x in range(COLS):
+        for g in range(3):
+            row = LINE * x + 8 * g
+            found = gathered(parts, x, g, 1, NODES)
+            if found is None:
+                field[row : row + 8, :] = jnp.zeros((8, 128), F32)
+                continue
+            mass_x = sum(weights[x - P_SIZE * e - 1] * element_width / 2.0
+                         for e in range(ELEMS) if 0 <= x - P_SIZE * e - 1 < NODES)
+            field[row : row + 8, :] = (
+                raw[row : row + 8, :] - found - (mass_shift[g] * np.float32(mass_x)) * total[row : row + 8, :])
+    exchange(2, field, RESIDUAL)
     solve(field, fix)
-    sent += exchange(3, fix, CORRECTION)
+    exchange(3, fix, CORRECTION)
     out_ref[...] = total[...] + fix[...]
-    for one in sent:
-        one.wait_send()
+    for number in range(4):
+        all_of(number, 208, 0).wait_send()
     for stage in range(2):
         for half in range(2):
-            copy = share(stage, half)
-            each_rank(lambda dz, group, copy=copy: copy(dz, group).wait_send())
+            bytes_of(stage, half).wait_send()
 
 
 def place_kernel(grid_ref, out_ref):
@@ -608,22 +638,25 @@
     vmem = pl.BlockSpec(memory_space=pltpu.VMEM)
     anywhere = pl.BlockSpec(memory_space=pl.ANY)
     tables = {name: jnp.asarray(table) for name, table in single.items()}
+    tables["stream"] = stream_speed.reshape(1152, 64)
+    tables["normal"] = normal_speed.reshape(1152, 64)
+    given = [tables[name] for name in TABLES]
     grid = pltpu.VMEM((GRID, 128), F32)
     flat = pltpu.VMEM((FLAT, 128), F32)
     solved = pl.pallas_call(
         functools.partial(step_kernel, lambdas_x, weights, heights),
         out_shape=jax.ShapeDtypeStruct((GRID, 128), F32),
-        in_specs=[vmem] * 3 + [anywhere] * len(TABLES),
+        in_specs=[anywhere] * len(TABLES),
         out_specs=vmem,
-        scratch_shapes=[pltpu.VMEM(single[name].shape, single[name].dtype) for name in TABLES] + [
+        scratch_shapes=[pltpu.VMEM(table.shape, table.dtype) for table in given] + [
             flat, flat, flat, flat,
             pltpu.VMEM((32, 16, 128), F32),
             pltpu.VMEM((4096, 32), F32),
             pltpu.VMEM((16, 128, 256), BF16),
-            pltpu.VMEM((2, SPECTRAL, WINDOW), BF16),
-            pltpu.VMEM((2, WINDOW, SPECTRAL), BF16),
-            pltpu.VMEM((2, OWN, OWN), BF16),
-            pltpu.VMEM((SPECTRAL, 128), F32),
+            pltpu.VMEM((2, 2, EXT_POINTS * 16, EXT_POINTS * 16), BF16),
+            pltpu.VMEM((2, 2, EXT_POINTS * 16, EXT_POINTS * 16), BF16),
+            pltpu.VMEM((2, 2, NODES * 16, NODES * 16), BF16),
+            pltpu.VMEM((2, EXT_POINTS * 16, 128), F32),
             grid, grid, grid, grid,
             pltpu.VMEM((4, 2, 48, 128), F32),
             pltpu.VMEM((4, 2, COLS, 128), F32),
@@ -632,15 +665,14 @@
             pltpu.VMEM((4, 2, COLS, 128), F32),
             pltpu.VMEM((4, 2, 8, 128), F32),
             pltpu.SemaphoreType.DMA((len(TABLES),)),
-            pltpu.SemaphoreType.DMA((4, 32)),
-            pltpu.SemaphoreType.DMA((4, 32)),
-            pltpu.SemaphoreType.DMA((4, 5)),
-            pltpu.SemaphoreType.DMA((4, 5)),
+            pltpu.SemaphoreType.DMA((4,)),
+            pltpu.SemaphoreType.DMA((4,)),
+            pltpu.SemaphoreType.DMA((4,)),
+            pltpu.SemaphoreType.DMA((4, 2)),
         ],
         compiler_params=pltpu.CompilerParams(collective_id=1, has_side_effects=True),
         name="step",
-    )(stream_speed.reshape(1152, 64), normal_speed.reshape(1152, 64), tables["lift"],
-      *[tables[name] for name in TABLES])
+    )(*given)
     placed = pl.pallas_call(
         place_kernel,
         out_shape=jax.ShapeDtypeStruct((1152, 128), F32),

time: 64.9 us -> 60.4 us (0.931)
  Pallas kernels: 64.5 us -> 60.3 us
    pallas_call x1, Pallas kernels: 62.5 us -> 58.2 us  [on_device(): pl.pallas_call(functools.partial(step_kernel, lambdas_x, weights, heights...]
where the time goes in v2:
time: 60.4 us; the launch traced here: 60.3 us
  Pallas kernels  60.3 us (100%)
    pallas_call x1, Pallas kernels, on_device(): pl.pallas_call(functools.partial(step_kernel, lambdas_x, weights, heights...  58.2 us
    pallas_call x1, Pallas kernels, on_device(): pl.pallas_call(place_kernel, out_shape=jax.ShapeDtypeStruct((1152, 128),...  2.05 us

profile of v2, /device:TPU:8, one launch (start us, length us, event | category | flops | bytes accessed | tf_op | source)
XLA Modules:
  0.0 60.3 jit_solution(1752662954525943077)
XLA Ops:
  0.0 58.2 %step.1.grid_ref = f32[1152,128]{1,0:T(8,128)} custom-call(f32[1152,64]{1,0:T(8,128)} %bitcast.3, f32[1152,64]{1,0:T(8,128)} %bitcast.4, bf16[1008,432]{1,0:T(8,128)(2,1)} %constant.28.clone.refs_2_, bf16[2,192,1008]{2,1,0:T(8,128)(2,1)} %constant.29.clone.refs_3_, f32[2,32,128]{2,1,0:T(8,128)} %constant.30.clone.refs_4_, ...), custom_call_target="tpu_custom_call" | custom-call | tf_op jit(solution)/shard_map/step/pallas_call | solution.py:646
  58.3 2.0 %place.1 = f32[1152,128]{1,0:T(8,128)} custom-call(f32[1152,128]{1,0:T(8,128)} %step.1.grid_ref), custom_call_target="tpu_custom_call" | custom-call | tf_op jit(solution)/shard_map/place/pallas_call | solution.py:676

commit v3 on v2

--- a/solution.py
+++ b/solution.py
@@ -184,6 +184,13 @@
 
 def dot_rows(left, right):
     return lax.dot_general(left, right, (((1,), (1,)), ((), ())), preferred_element_type=F32)
+
+
+SMALL = (("wave", 64, 128), ("twist", 128, 128), ("in_x", 16, 224), ("in_y", 64, 224), ("out_x", 16, 224),
+         ("out_y", 64, 224), ("own_kx", 16, 192), ("own_my", 64, 192), ("own_wx", 16, 192), ("own_ky", 64, 192),
+         ("mass", 48, 128), ("lam", 64, 128))
+SMALL_AT = {entry[0]: sum(other[1] for other in SMALL[:at]) for at, entry in enumerate(SMALL)}
+SMALL_WIDTH = {name: width for name, _, width in SMALL}
 
 
 @functools.cache
@@ -260,12 +267,14 @@
     own_wx = np.kron(np.diag(weights) * (element_width / 2.0), ones_line)
     own_ky = np.tile(row_stiff, (1, 1, 1, NODES))
     wide = np.ones((1, 1, 128))
-    single = dict(lift=lift_cat, back=back_cat)
-    single.update({name: np.asarray(table, np.float32) for name, table in dict(
-        wave=wave, twist=twist,
-        in_x=in_x, in_y=in_y, out_x=out_x, out_y=out_y,
-        own_kx=own_kx, own_my=own_my, own_wx=own_wx, own_ky=own_ky,
-        mass=line_mass[:, :, None] * wide, lam=line_lambda[..., None] * wide[None]).items()})
+    named = dict(
+        wave=wave, twist=twist, in_x=in_x, in_y=in_y, out_x=out_x, out_y=out_y, own_kx=own_kx, own_my=own_my,
+        own_wx=own_wx, own_ky=own_ky, mass=line_mass[:, :, None] * wide, lam=line_lambda[..., None] * wide[None])
+    small = np.zeros((sum(rows for _, rows, _ in SMALL), 256), np.float32)
+    for name, rows, width in SMALL:
+        table = named[name].reshape(-1, width)
+        small[SMALL_AT[name] : SMALL_AT[name] + table.shape[0], :width] = table
+    single = dict(lift=lift_cat, back=back_cat, small=small)
     return single, np.asarray(lambdas_x), np.asarray(weights), np.asarray(heights)
 
 
@@ -312,8 +321,7 @@
 
 RESIDUAL = ((1, 44, 45, 0), (21, 22), (1, 0))
 CORRECTION = ((0, 45, 44, 1), (22, 21), (0, 1))
-TABLES = ("stream", "normal", "lift", "back", "wave", "twist", "in_x", "in_y", "out_x", "out_y", "own_kx", "own_my", "own_wx",
-          "own_ky", "mass", "lam")
+TABLES = ("stream", "normal", "lift", "back", "small")
 
 
 def step_kernel(lambdas_x, weights, heights, *refs):
@@ -472,17 +480,24 @@
             modal_out[base + 16 * q : base + 16 * q + 16, :] = jnp.where(even, turned[:16], turned[16:])
 
     carried = store_weak(0, advect(0), None)
-    store_weak(1, advect(1), carried)
     pl.semaphore_wait(barrier, RANKS - 1 + 5)
     send(0, 0)
+    store_weak(1, advect(1), carried)
     send(0, 1)
+
+    def part(name, start, count):
+        return held["small"][pl.ds(SMALL_AT[name] + start, count), : SMALL_WIDTH[name]]
+
+    def row_part(name, f):
+        start = pl.multiple_of(SMALL_AT[name] + 16 * (ROWS_DEV * ey + f), 16)
+        return held["small"][pl.ds(start, 16), : SMALL_WIDTH[name]]
 
     for load in loads[4:]:
         load.wait()
     for rp in range(16):
         for at in range(4):
-            pair = held["twist"][rp, 2 * at : 2 * at + 2, :]
-            high, low = split(held["wave"][0] * pair[:1] + held["wave"][1] * pair[1:])
+            pair = part("twist", 8 * rp + 2 * at, 2)
+            high, low = split(part("wave", 0, 32) * pair[:1] + part("wave", 32, 32) * pair[1:])
             fourier[rp, 32 * at : 32 * at + 32, :128] = high
             fourier[rp, 32 * at : 32 * at + 32, 128:] = low
     lane = lax.broadcasted_iota(jnp.int32, (1, 128), 1)
@@ -491,18 +506,18 @@
     for f in range(ROWS_DEV):
         for i in range(EXT_POINTS):
             rows = slice(16 * i, 16 * i + 16)
-            high, low = split(held["in_x"][i : i + 1, :] * held["in_y"][ey, f])
+            high, low = split(part("in_x", i, 1) * row_part("in_y", f))
             inward[f, 0, rows, :], inward[f, 1, rows, :] = high, low
-            high, low = split(held["out_x"][i : i + 1, :] * held["out_y"][ey, f])
+            high, low = split(part("out_x", i, 1) * row_part("out_y", f))
             outward[f, 0, rows, :], outward[f, 1, rows, :] = high, low
-            inverse[f, rows, :] = 1.0 / (held["lam"][ey, f] + (shift + np.float32(lambdas_x[i])))
+            inverse[f, rows, :] = 1.0 / (row_part("lam", f) + (shift + np.float32(lambdas_x[i])))
         for a in range(NODES):
             rows = slice(16 * a, 16 * a + 16)
             high, low = split(
-                held["own_kx"][a : a + 1, :] * held["own_my"][ey, f]
-                + held["own_wx"][a : a + 1, :] * held["own_ky"][ey, f])
+                part("own_kx", a, 1) * row_part("own_my", f)
+                + part("own_wx", a, 1) * row_part("own_ky", f))
             local[f, 0, rows, :], local[f, 1, rows, :] = high, low
-    mass_shift = [held["mass"][ey, 8 * g : 8 * g + 8, :] * shift for g in range(3)]
+    mass_shift = [held["small"][pl.ds(pl.multiple_of(SMALL_AT["mass"] + LINE * ey + 8 * g, 8), 8), :128] * shift for g in range(3)]
     raw[...] = jnp.zeros((GRID, 128), F32)
 
     for half in range(2):
@@ -636,7 +651,7 @@
 def on_device(stream_speed, normal_speed):
     single, lambdas_x, weights, heights = all_tables()
     vmem = pl.BlockSpec(memory_space=pltpu.VMEM)
-    anywhere = pl.BlockSpec(memory_space=pl.ANY)
+    remote = pl.BlockSpec(memory_space=pltpu.HBM)
     tables = {name: jnp.asarray(table) for name, table in single.items()}
     tables["stream"] = stream_speed.reshape(1152, 64)
     tables["normal"] = normal_speed.reshape(1152, 64)
@@ -646,7 +661,7 @@
     solved = pl.pallas_call(
         functools.partial(step_kernel, lambdas_x, weights, heights),
         out_shape=jax.ShapeDtypeStruct((GRID, 128), F32),
-        in_specs=[anywhere] * len(TABLES),
+        in_specs=[remote] * len(TABLES),
         out_specs=vmem,
         scratch_shapes=[pltpu.VMEM(table.shape, table.dtype) for table in given] + [
             flat, flat, flat, flat,
@@ -670,7 +685,8 @@
             pltpu.SemaphoreType.DMA((4,)),
             pltpu.SemaphoreType.DMA((4, 2)),
         ],
-        compiler_params=pltpu.CompilerParams(collective_id=1, has_side_effects=True),
+        compiler_params=pltpu.CompilerParams(
+            collective_id=1, has_side_effects=True, vmem_limit_bytes=54500 * 1024),
         name="step",
     )(*given)
     placed = pl.pallas_call(
@@ -678,6 +694,7 @@
         out_shape=jax.ShapeDtypeStruct((1152, 128), F32),
         in_specs=[vmem],
         out_specs=vmem,
+        compiler_params=pltpu.CompilerParams(vmem_limit_bytes=8 * 2**20),
         name="place",
     )(solved)
     return placed.reshape(12, 12, 4, 2, 128)

time: 60.4 us -> 58.1 us (0.962)
  Pallas kernels: 60.3 us -> 57.9 us
    pallas_call x1, Pallas kernels: 58.2 us -> 57 us  [on_device(): pl.pallas_call(functools.partial(step_kernel, lambdas_x, weights, heights...]
    pallas_call x1, Pallas kernels: 2.05 us -> 0.98 us  [on_device(): pl.pallas_call(place_kernel, out_shape=jax.ShapeDtypeStruct((1152, 128),...]
where the time goes in v3:
time: 58.1 us; the launch traced here: 57.9 us
  Pallas kernels  57.9 us (100%)
    pallas_call x1, Pallas kernels, on_device(): pl.pallas_call(functools.partial(step_kernel, lambdas_x, weights, heights...  57 us

profile of v3, /device:TPU:8, one launch (start us, length us, event | category | flops | bytes accessed | tf_op | source)
XLA Modules:
  0.0 57.9 jit_solution(5339491666507446491)
XLA Ops:
  0.0 57.0 %step.1.grid_ref = f32[1152,128]{1,0:T(8,128)S(1)} custom-call(f32[1152,64]{1,0:T(8,128)} %bitcast.3, f32[1152,64]{1,0:T(8,128)} %bitcast.4, bf16[1008,432]{1,0:T(8,128)(2,1)} %constant.6.clone.refs_2_, bf16[2,192,1008]{2,1,0:T(8,128)(2,1)} %constant.7.clone.refs_3_, f32[624,256]{1,0:T(8,128)} %constant.8.clone.refs_4_), custom_call_target="tpu_custom_call" | custom-call | tf_op jit(solution)/shard_map/step/pallas_call | solution.py:661
  57.0 1.0 %place.1 = f32[1152,128]{1,0:T(8,128)} custom-call(f32[1152,128]{1,0:T(8,128)S(1)} %step.1.grid_ref), custom_call_target="tpu_custom_call" | custom-call | tf_op jit(solution)/shard_map/place/pallas_call | solution.py:692

commit v4 on v3

--- a/solution.py
+++ b/solution.py
@@ -337,23 +337,18 @@
     low_side = ey == 0
     my_z, my_y, my_c = me // 8, lax.rem(me // 2, 4), lax.rem(me, 2)
 
+    z_part = [8 * lax.rem(my_z + dz, 4) for dz in range(4)]
+    yc_part = [2 * lax.rem(my_y + group // 2, 4) + lax.rem(my_c + group % 2, 2) for group in range(8)]
+
     def rank(dz, group):
-        dy, dc = group // 2, lax.rem(group, 2)
-        return 8 * lax.rem(my_z + dz, 4) + 2 * lax.rem(my_y + dy, 4) + lax.rem(my_c + dc, 2)
+        return z_part[dz] + yc_part[group]
 
     def each_rank(act):
-        def apart(i, carry):
+        for group in (4, 5, 6, 7, 2, 3, 1, 0):
             for dz in (2, 1, 3):
-                act(dz, lax.rem(i + 4, 8))
-            return carry
-
-        def beside(i, carry):
-            act(0, i)
-            return carry
-
-        lax.fori_loop(0, 8, apart, 0)
-        lax.fori_loop(4, 8, beside, 0)
-        lax.fori_loop(1, 4, beside, 0)
+                act(dz, group)
+        for group in (4, 5, 6, 7, 2, 3, 1):
+            act(0, group)
 
     loads = [pltpu.make_async_copy(source, held[name], table_sem.at[at])
              for at, (name, source) in enumerate(zip(TABLES, sources, strict=True))]
@@ -534,7 +529,7 @@
             src_ref=raw.at[pl.ds(0, rows)], dst_ref=raw.at[pl.ds(0, rows)], send_sem=send_sem.at[number],
             recv_sem=recv_sem.at[number, at], device_id=peers[2], device_id_type=MESH)
 
-    def exchange(number, grid, kind):
+    def exchange(number, grid, kind, landing=None, meanwhile=None):
         (to_left, to_right, from_right, from_left), lower, upper = kind
         zero = jnp.zeros((4, 128), F32)
         pieces = []
@@ -559,9 +554,13 @@
             pltpu.make_async_remote_copy(
                 src_ref=source, dst_ref=target, send_sem=send_sem.at[number],
                 recv_sem=recv_sem.at[number, at // 3], device_id=peer, device_id_type=MESH).start()
+        if landing is None:
+            landing = grid
+        if meanwhile is not None:
+            meanwhile()
         all_of(number, 96, 1).wait_recv()
-        grid[LINE * from_right : LINE * from_right + 48, :] += side_in[number, 0]
-        grid[LINE * from_left : LINE * from_left + 48, :] += side_in[number, 1]
+        landing[LINE * from_right : LINE * from_right + 48, :] += side_in[number, 0]
+        landing[LINE * from_left : LINE * from_left + 48, :] += side_in[number, 1]
         all_of(number, 112, 0).wait_recv()
         zeros = jnp.zeros((COLS, 128), F32)
         for step in range(2):
@@ -574,8 +573,8 @@
             added = rows[0] + rows[1] + rows[2]
             where_low = pl.ds(lower[1] + step, COLS, stride=LINE)
             where_up = pl.ds(upper[1] + step, COLS, stride=LINE)
-            grid[where_low, :] += jnp.where(low_side, added, zeros)
-            grid[where_up, :] += jnp.where(low_side, zeros, added)
+            landing[where_low, :] += jnp.where(low_side, added, zeros)
+            landing[where_up, :] += jnp.where(low_side, zeros, added)
 
     def rows_of(source, f, first, count):
         return jnp.concatenate(
@@ -611,8 +610,13 @@
                 row = LINE * x + 8 * g
                 target[row : row + 8, :] = jnp.zeros((8, 128), F32) if found is None else found
 
-    field[...] = raw[...]
-    exchange(0, field, RESIDUAL)
+    def copy_raw():
+        field[...] = raw[...]
+
+    def add_up():
+        out_ref[...] = total[...] + fix[...]
+
+    exchange(0, raw, RESIDUAL, field, copy_raw)
     solve(field, total)
     exchange(1, total, CORRECTION)
     parts = [apply(local.at[f], rows_of(total, f, 1, NODES)) for f in range(ROWS_DEV)]
@@ -629,8 +633,7 @@
                 raw[row : row + 8, :] - found - (mass_shift[g] * np.float32(mass_x)) * total[row : row + 8, :])
     exchange(2, field, RESIDUAL)
     solve(field, fix)
-    exchange(3, fix, CORRECTION)
-    out_ref[...] = total[...] + fix[...]
+    exchange(3, fix, CORRECTION, out_ref, add_up)
     for number in range(4):
         all_of(number, 208, 0).wait_send()
     for stage in range(2):

time: 58.1 us -> 56.6 us (0.974); the launches traced: 57.9 us -> 55.7 us
  Pallas kernels: 57.9 us -> 55.7 us
    pallas_call x1, Pallas kernels: 57 us -> 54.7 us  [on_device(): pl.pallas_call(functools.partial(step_kernel, lambdas_x, weights, heights...]
where the time goes in v4:
time: 56.6 us; the launch traced here: 55.7 us
  Pallas kernels  55.7 us (98%)
    pallas_call x1, Pallas kernels, on_device(): pl.pallas_call(functools.partial(step_kernel, lambdas_x, weights, heights...  54.7 us

profile of v4, /device:TPU:8, one launch (start us, length us, event | category | flops | bytes accessed | tf_op | source)
XLA Modules:
  0.0 55.7 jit_solution(5038029456860105689)
XLA Ops:
  0.0 54.7 %step.1.grid_ref = f32[1152,128]{1,0:T(8,128)S(1)} custom-call(f32[1152,64]{1,0:T(8,128)} %bitcast.3, f32[1152,64]{1,0:T(8,128)} %bitcast.4, bf16[1008,432]{1,0:T(8,128)(2,1)} %constant.6.clone.refs_2_, bf16[2,192,1008]{2,1,0:T(8,128)(2,1)} %constant.7.clone.refs_3_, f32[624,256]{1,0:T(8,128)} %constant.8.clone.refs_4_), custom_call_target="tpu_custom_call" | custom-call | tf_op jit(solution)/shard_map/step/pallas_call | solution.py:664
  54.7 1.0 %place.1 = f32[1152,128]{1,0:T(8,128)} custom-call(f32[1152,128]{1,0:T(8,128)S(1)} %step.1.grid_ref), custom_call_target="tpu_custom_call" | custom-call | tf_op jit(solution)/shard_map/place/pallas_call | solution.py:695
